TPU v7x, 512 devices: a whole 4x4x16 slice. The times are simulated.
512 devices in a mesh: gx: 32 (over z, core), gy: 16 (over y, x).
Axes of the slice: x: 4, y: 4, z: 16, core: 2. Of those that a mesh axis runs over, the one named last changes fastest.
Arguments:
- thermal_anomaly: float32 [16, 128, 4096], P(None, 'gy', 'gx'), may hold values from -6 to 6
- saltiness_anomaly: float32 [16, 128, 4096], P(None, 'gy', 'gx'), may hold values from -6 to 6
- zonal_volume_rate: float32 [16, 128, 4096], P(None, 'gy', 'gx'), may hold values from -0.12 to 0.12
- meridional_volume_rate: float32 [16, 128, 4096], P(None, 'gy', 'gx'), may hold values from -0.12 to 0.12
- sideways_diffusivity_factor: float32 [128, 4096], P('gy', 'gx'), may hold values from 0.02 to 0.13
- stratum_interface_mixing: float32 [15, 128, 4096], P(None, 'gy', 'gx'), may hold values from 0.05 to 20
- flooded_strata: int32 [128, 4096], P('gy', 'gx'), may hold values from 0 to 16
- patch_sea_source: int32 [16, 65536], P('gy', 'gx'), may hold values from 0 to 1023, as said below
- patch_sky_target: int32 [16, 65536], P('gy', 'gx'), may hold values from 0 to 8191, as said below
- patch_measure_pointer: int32 [16, 65536], P('gy', 'gx'), may hold values from 0 to 63
- patch_measures: float32 [64], replicated, may hold values from 0.05 to 1
- holder_ordering: int32 [16, 8192], P('gy'), may hold values from 0 to 8191, as said below
Outputs:
- temperature_next: float32 [16, 128, 4096], P(None, 'gy', 'gx')
- salinity_next: float32 [16, 128, 4096], P(None, 'gy', 'gx')
- air_sums: float32 [2, 16, 8192], P(None, 'gy', 'gx')
Inputs may be any that keep to these rules, and one draw needn't show every extreme that they name: `patch_sea_source`: Row-major index of the ocean cell within the 8 x 128 tile of the device that holds the entry. `patch_sky_target`: Row-major index over the atmosphere cells of the row of tiles, half of 8 rows by half of 4096 columns, each covering 2 x 2 ocean cells; it is the cell containing the intersection's ocean cell, its eastern neighbour (periodic), or its northern or southern neighbour within the row of tiles. `holder_ordering`: each row is a permutation. Call the atmosphere cells of columns q * 64 to (q + 1) * 64 - 1 of a row the cells over tile column q; for every q and every owner o (place // 256 = o), exactly 8 cells over tile column q have owner o.
All inputs are finite; a program needn't handle non-finite values.
Results may differ from a plain program's by a relative error of at most 0.00002.
Values sent between devices are 32-bit elements; how exact they have to be, the bound alone decides.
No kernel may reach another device: no remote copies, remote signals or barrier semaphores. Data moves between devices by JAX's collectives and lax.ppermute only.
A program may use at most 64 MiB of HBM per device.

v0:
```python
import jax
import jax.numpy as jnp
from jax import lax
from jax.sharding import PartitionSpec as P

NSUB = 4


def with_halo(cells, sides, width):
    for axis, dim in sides:
        count = lax.axis_size(axis)
        head = lax.slice_in_dim(cells, 0, width, axis=dim)
        tail = lax.slice_in_dim(cells, cells.shape[dim] - width, cells.shape[dim], axis=dim)
        cells = jnp.concatenate(
            [
                lax.ppermute(tail, axis, [(i, (i + 1) % count) for i in range(count)]),
                cells,
                lax.ppermute(head, axis, [((i + 1) % count, i) for i in range(count)]),
            ],
            axis=dim,
        )
    return cells


def advance(quantity, east_vel, north_vel, diffusivity, wetness):
    open_east = wetness[:, :, :-1] * wetness[:, :, 1:]
    kappa_east = 0.5 * (diffusivity[:, :-1] + diffusivity[:, 1:])
    speed = east_vel[:, :, :-1]
    left = quantity[..., :-1]
    right = quantity[..., 1:]
    flux_east = open_east * (
        jnp.maximum(speed, 0.0) * left
        + jnp.minimum(speed, 0.0) * right
        - kappa_east * (right - left)
    )
    open_north = wetness[:, :-1, :] * wetness[:, 1:, :]
    kappa_north = 0.5 * (diffusivity[:-1, :] + diffusivity[1:, :])
    northward = north_vel[:, :-1, :]
    lower = quantity[:, :, :-1, :]
    upper = quantity[:, :, 1:, :]
    flux_north = open_north * (
        jnp.maximum(northward, 0.0) * lower
        + jnp.minimum(northward, 0.0) * upper
        - kappa_north * (upper - lower)
    )
    across = flux_east[..., 1:] - flux_east[..., :-1]
    along = flux_north[:, :, 1:, :] - flux_north[:, :, :-1, :]
    return quantity[:, :, 1:-1, 1:-1] - (across[:, :, 1:-1, :] + along[:, :, :, 1:-1])


def column_solve(quantity, vertical, wetness):
    coupling = vertical * wetness[:-1] * wetness[1:]
    strata_stack = quantity.shape[1]
    ratios = []
    partial_value = []
    for level in range(strata_stack):
        below = coupling[level] if level < strata_stack - 1 else 0.0
        above = coupling[level - 1] if level > 0 else 0.0
        diagonal = 1.0 + above + below
        if level == 0:
            denom = diagonal
            value = quantity[:, 0]
        else:
            denom = diagonal + above * ratios[-1]
            value = quantity[:, level] + above * partial_value[-1]
        ratios.append(-below / denom)
        partial_value.append(value / denom)
    result = [None] * strata_stack
    result[strata_stack - 1] = partial_value[strata_stack - 1]
    for level in range(strata_stack - 2, -1, -1):
        result[level] = partial_value[level] - ratios[level] * result[level + 1]
    return jnp.stack(result, axis=1)


def shrink(array):
    return array[..., 1:-1, 1:-1]


def shards(
    thermal_anomaly,
    saltiness_anomaly,
    zonal_volume_rate,
    meridional_volume_rate,
    sideways_diffusivity_factor,
    stratum_interface_mixing,
    flooded_strata,
    patch_sea_source,
    patch_sky_target,
    patch_measure_pointer,
    patch_measures,
    holder_ordering,
):
    strata_stack, block_meridional_span, block_zonal_extent = thermal_anomaly.shape
    quantity = jnp.stack([thermal_anomaly, saltiness_anomaly])
    statics = jnp.concatenate(
        [
            zonal_volume_rate,
            meridional_volume_rate,
            sideways_diffusivity_factor[None],
            flooded_strata.astype(jnp.float32)[None],
        ],
        axis=0,
    )
    rimmed = with_halo(statics, (("gx", 2), ("gy", 1)), 2)
    band_rows = block_meridional_span * lax.axis_size("gy")
    global_rows = (
        lax.axis_index("gy") * block_meridional_span - 2 + jnp.arange(block_meridional_span + 4)
    )
    inside = (global_rows >= 0) & (global_rows < band_rows)
    depth_ext = jnp.where(inside[:, None], rimmed[2 * strata_stack + 1], 0.0)
    wet_ext = (jnp.arange(strata_stack, dtype=jnp.float32)[:, None, None] < depth_ext[None]).astype(
        jnp.float32
    )
    east_ext = rimmed[:strata_stack]
    north_ext = rimmed[strata_stack : 2 * strata_stack]
    kappa_ext = rimmed[2 * strata_stack]
    east_inner = shrink(east_ext)
    north_inner = shrink(north_ext)
    kappa_inner = shrink(kappa_ext)
    wet_inner = shrink(wet_ext)
    for repeat in range(NSUB):
        widened = with_halo(quantity, (("gx", 3), ("gy", 2)), 1)
        quantity = advance(widened, east_inner, north_inner, kappa_inner, wet_inner)
    wetness = wet_ext[:, 2:-2, 2:-2]
    quantity = column_solve(quantity, stratum_interface_mixing, wetness)
    surface = quantity[:, 0].reshape(2, block_meridional_span * block_zonal_extent)
    wet_top = wetness[0].reshape(-1)
    cells = patch_sea_source[0]
    weights = jnp.take(patch_measures, patch_measure_pointer[0]) * jnp.take(wet_top, cells)
    terms = jnp.take(surface, cells, axis=1) * weights[None]
    row_cells = holder_ordering.shape[1]
    places = jnp.take(holder_ordering[0], patch_sky_target[0])
    partial_sums = jnp.zeros((2, row_cells), jnp.float32).at[:, places].add(terms)
    owned = lax.psum_scatter(partial_sums, "gx", scatter_dimension=1, tiled=True)
    return (quantity[0], quantity[1], owned[:, None, :])


def solution(mesh):
    placed = (
        P(None, "gy", "gx"),
        P(None, "gy", "gx"),
        P(None, "gy", "gx"),
        P(None, "gy", "gx"),
        P("gy", "gx"),
        P(None, "gy", "gx"),
        P("gy", "gx"),
        P("gy", "gx"),
        P("gy", "gx"),
        P("gy", "gx"),
        P(),
        P("gy", None),
    )
    return jax.shard_map(
        shards,
        mesh=mesh,
        in_specs=placed,
        out_specs=(P(None, "gy", "gx"), P(None, "gy", "gx"), P(None, "gy", "gx")),
        check_vma=False,
    )
```

profile of v0, /device:TPU:24, one launch (start us, length us, event | category | flops | bytes accessed | tf_op | source)
XLA Modules:
  0.0 311.0 jit_solution(2988093780018918888)
XLA Ops:
  7.2 0.7 convert_bitcast_fusion
  7.9 0.9 pad_maximum_fusion.16
  8.9 8.9 %collective-permute-start.1 = (f32[34,8,2]{2,1,0:T(8,128)S(1)}, f32[34,8,2]{2,1,0:T(8,128)S(1)}, u32[]{:S(2)}, u32[]{:S(2)}) collective-permute-start(f32[34,8,2]{2,1,0:T(8,128)S(1)} %get-tuple-element.148), channel_id=1, source_target_pairs={{16,0},{32,16},{48,32},{64,48},{80,64},{96,80},{112,96},{128,112},... | collective-permute-start | bytes 6536 | tf_op jit(solution)/shard_map/ppermute | solution.py:18
  17.9 1.0 fusion.8
  18.9 2.9 collective-permute-start.5
  21.9 1.6 fusion.83
  23.5 2.1 fusion.80
  25.6 2.1 fusion.81
  27.6 2.1 fusion.82
  29.7 0.7 compare_select_fusion.3
  30.4 0.7 compare_and_fusion
  31.1 0.7 compare_select_fusion.5
  31.9 11.8 %gather_fusion = s32[2048]{0:T(1024)S(1)} fusion(s32[8192]{0:T(1024)S(1)} %bitcast.395, s32[2048]{0:T(1024)S(1)} %get-tuple-element.291), kind=kCustom, calls=%fused_computation | custom fusion | bytes 24576 | tf_op jit(solution)/shard_map/jit(_take)/gather | solution.py:132
  43.8 4.5 %compare_select_fusion.6 = (f32[2048,1]{0,1:T(1,128)S(1)}, s32[2048,1]{0,1:T(1,128)S(1)}) fusion(f32[]{:T(128)} %bitcast.166, f32[]{:T(128)} %bitcast.167, f32[]{:T(128)} %bitcast.168, f32[]{:T(128)} %bitcast.169, f32[]{:T(128)} %bitcast.170, f32[]{:T(128)} %bitcast.172, f32[]{:T(128)} %bitcast.171, s32[1,2048]{1,0:T(1,128)S(1)} %copy-done.8), kind=kLoop, calls=%fused_computation.172 | loop fusion | flops 30720 | bytes 24604 | tf_op jit(solution)/shard_map/jit(_take)/gather | solution.py:129
  48.3 1.4 compare_reduce_fusion.56
  49.7 35.7 %select_select_fusion = f32[2048]{0:T(1024)S(1)} fusion(pred[2048]{0:T(1024)(128)(4,1)S(1)} %get-tuple-element.68, pred[2048]{0:T(1024)(128)(4,1)S(1)} %get-tuple-element.67, pred[2048]{0:T(1024)(128)(4,1)S(1)} %get-tuple-element.66, pred[2048]{0:T(1024)(128)(4,1)S(1)} %get-tuple-element.65, pred[2048]{0:T(1024)(128)(4,1)S(1)} %get-tuple-element.64, ...), kind=kLoop, calls=%fused_computation.221 | loop fusion | flops 116736 | bytes 133348 | tf_op jit(solution)/shard_map/jit(_take)/gather | solution.py:129
  85.7 3.4 %collective-permute-start.6 = (f32[2,16,1,130]{3,2,1,0:T(1,128)S(1)}, f32[2,16,1,130]{3,2,1,0:T(1,128)S(1)}, u32[]{:S(2)}, u32[]{:S(2)}) collective-permute-start(f32[2,16,1,130]{3,2,1,0:T(1,128)S(1)} %get-tuple-element.145), channel_id=1, source_target_pairs={{0,1},{1,2},{2,3},{3,4},{4,5},{5,6},{6,7},{7,8},{8,9},{9,10},{10,1... | collective-permute-start | bytes 49928 | tf_op jit(solution)/shard_map/ppermute | solution.py:16
  89.2 4.6 %collective-permute-start.7 = (f32[2,16,1,130]{3,2,1,0:T(1,128)S(1)}, f32[2,16,1,130]{3,2,1,0:T(1,128)S(1)}, u32[]{:S(2)}, u32[]{:S(2)}) collective-permute-start(f32[2,16,1,130]{3,2,1,0:T(1,128)S(1)} %get-tuple-element.146), channel_id=1, source_target_pairs={{1,0},{2,1},{3,2},{4,3},{5,4},{6,5},{7,6},{8,7},{9,8},{10,9},{11,1... | collective-permute-start | bytes 49928 | tf_op jit(solution)/shard_map/ppermute | solution.py:18
  93.8 0.3 pad_maximum_fusion.22
  94.1 1.9 collective-permute-start.2
  96.0 6.0 %collective-permute-start.3 = (f32[34,2,132]{2,1,0:T(2,128)S(1)}, f32[34,2,132]{2,1,0:T(2,128)S(1)}, u32[]{:S(2)}, u32[]{:S(2)}) collective-permute-start(f32[34,2,132]{2,1,0:T(2,128)S(1)} %get-tuple-element.138), channel_id=1, source_target_pairs={{1,0},{2,1},{3,2},{4,3},{5,4},{6,5},{7,6},{8,7},{9,8},{10,9},{11,1... | collective-permute-start | bytes 107720 | tf_op jit(solution)/shard_map/ppermute | solution.py:18
  102.4 1.6 collective-permute-done.3
  104.0 0.3 pad_maximum_fusion
  105.6 0.4 subtract_multiply_fusion.6
  106.8 2.9 collective-permute-start.9
  109.7 8.6 %gather_fusion.1 = f32[2048]{0:T(1024)S(1)} fusion(f32[1024]{0:T(1024)S(1)} %slice_bitcast_fusion.19, s32[2048]{0:T(1024)S(1)} %get-tuple-element.290), kind=kCustom, calls=%fused_computation.2 | custom fusion | bytes 24576 | tf_op jit(solution)/shard_map/jit(_take)/gather | solution.py:129
  118.7 1.9 collective-permute-start.10
  120.6 6.4 %collective-permute-start.11 = (f32[2,16,1,130]{3,2,1,0:T(1,128)S(1)}, f32[2,16,1,130]{3,2,1,0:T(1,128)S(1)}, u32[]{:S(2)}, u32[]{:S(2)}) collective-permute-start(f32[2,16,1,130]{3,2,1,0:T(1,128)S(1)} %get-tuple-element.144), channel_id=1, source_target_pairs={{1,0},{2,1},{3,2},{4,3},{5,4},{6,5},{7,6},{8,7},{9,8},{10,9},{11,1... | collective-permute-start | bytes 49928 | tf_op jit(solution)/shard_map/ppermute | solution.py:18
  127.0 1.5 collective-permute-done.11
  128.6 0.4 subtract_multiply_fusion.4
  129.0 0.3 pad_maximum_fusion.3
  130.0 2.9 collective-permute-start.13
  133.0 2.6 collective-permute-done.12
  135.9 4.8 %collective-permute-start.14 = (f32[2,16,1,130]{3,2,1,0:T(1,128)S(1)}, f32[2,16,1,130]{3,2,1,0:T(1,128)S(1)}, u32[]{:S(2)}, u32[]{:S(2)}) collective-permute-start(f32[2,16,1,130]{3,2,1,0:T(1,128)S(1)} %get-tuple-element.141), channel_id=1, source_target_pairs={{0,1},{1,2},{2,3},{3,4},{4,5},{5,6},{6,7},{7,8},{8,9},{9,10},{10,1... | collective-permute-start | bytes 49928 | tf_op jit(solution)/shard_map/ppermute | solution.py:16
  140.7 3.5 %collective-permute-start.15 = (f32[2,16,1,130]{3,2,1,0:T(1,128)S(1)}, f32[2,16,1,130]{3,2,1,0:T(1,128)S(1)}, u32[]{:S(2)}, u32[]{:S(2)}) collective-permute-start(f32[2,16,1,130]{3,2,1,0:T(1,128)S(1)} %get-tuple-element.142), channel_id=1, source_target_pairs={{1,0},{2,1},{3,2},{4,3},{5,4},{6,5},{7,6},{8,7},{9,8},{10,9},{11,1... | collective-permute-start | bytes 49928 | tf_op jit(solution)/shard_map/ppermute | solution.py:18
  144.2 2.3 collective-permute-done.15
  146.5 0.4 subtract_multiply_fusion.2
  147.0 0.3 pad_maximum_fusion.5
  147.9 2.9 collective-permute-start.17
  150.9 2.6 collective-permute-done.16
  153.8 5.2 %collective-permute-start.18 = (f32[2,16,1,130]{3,2,1,0:T(1,128)S(1)}, f32[2,16,1,130]{3,2,1,0:T(1,128)S(1)}, u32[]{:S(2)}, u32[]{:S(2)}) collective-permute-start(f32[2,16,1,130]{3,2,1,0:T(1,128)S(1)} %get-tuple-element.139), channel_id=1, source_target_pairs={{0,1},{1,2},{2,3},{3,4},{4,5},{5,6},{6,7},{7,8},{8,9},{9,10},{10,1... | collective-permute-start | bytes 49928 | tf_op jit(solution)/shard_map/ppermute | solution.py:16
  159.0 2.9 collective-permute-start.19
  162.0 2.9 collective-permute-done.19
  164.8 0.4 subtract_multiply_fusion
  166.9 19.5 %scatter_custom_fusion = f32[2,8192]{0,1:T(8,128)} fusion(s32[2048]{0:T(1024)S(1)} %bitcast.450, f32[]{:T(128)} %constant.43.clone.1, f32[2048]{0:T(1024)S(1)} %bitcast.443, f32[]{:T(128)} %constant.78.clone.1, pred[2048]{0:T(1024)(128)(4,1)S(1)} %compare_and_fusion, f32[2,1024]{0,1:T(8,128)S(1)} %copy.49, s32[2048]{0:T(1024)S(1)} %get-tuple-element.290), kind=kCustom, calls=%fused_computation.4 | custom fusion | flops 12288 | bytes 608264 | tf_op jit(solution)/shard_map/scatter-add | solution.py:133
  186.4 0.7 slice_bitcast_fusion
  187.1 115.5 %reduce-scatter.2.cloned.1.call-done = f32[2,256]{0,1:T(8,128)} async-done(((f32[2,8192]{0,1:T(8,128)}), f32[2,256]{0,1:T(8,128)}) %reduce-scatter.2.cloned.1.call-update) | async-done | bytes 2064 | tf_op jit(solution)/shard_map/reduce_scatter | solution.py:134
  302.6 1.6 copy.50
  (114 shorter events, 6.7 us)
Async XLA Ops:
  7.2 24.7 %copy-start = (s32[1,8192]{1,0:T(1,128)S(1)}, s32[1,8192]{1,0:T(1,128)}, u32[]{:S(2)}) copy-start(s32[1,8192]{1,0:T(1,128)} %param.23) | copy-start | bytes 98308
  7.2 295.4 %reduce-scatter.2.cloned.1.call-start = ((), (), s32[]{:S(2)}) async-start(), calls=%async_computation.1 | async-start | bytes 4325376 | tf_op jit(solution)/shard_map/reduce_scatter | solution.py:134
  8.9 84.8 %collective-permute-start = (f32[34,8,2]{2,1,0:T(8,128)S(1)}, f32[34,8,2]{2,1,0:T(8,128)S(1)}, u32[]{:S(2)}, u32[]{:S(2)}) collective-permute-start(f32[34,8,2]{2,1,0:T(8,128)S(1)} %get-tuple-element.147), channel_id=1, source_target_pairs={{0,16},{16,32},{32,48},{48,64},{64,80},{80,96},{96,112},{112,128},... | collective-permute-start | bytes 6536 | tf_op jit(solution)/shard_map/ppermute | solution.py:16
  8.9 84.8 %collective-permute-start.1 = (f32[34,8,2]{2,1,0:T(8,128)S(1)}, f32[34,8,2]{2,1,0:T(8,128)S(1)}, u32[]{:S(2)}, u32[]{:S(2)}) collective-permute-start(f32[34,8,2]{2,1,0:T(8,128)S(1)} %get-tuple-element.148), channel_id=1, source_target_pairs={{16,0},{32,16},{48,32},{64,48},{80,64},{96,80},{112,96},{128,112},... | collective-permute-start | bytes 6536 | tf_op jit(solution)/shard_map/ppermute | solution.py:18
  18.9 66.5 %collective-permute-start.4 = (f32[2,16,8,1]{3,2,1,0:T(8,128)S(1)}, f32[2,16,8,1]{3,2,1,0:T(8,128)S(1)}, u32[]{:S(2)}, u32[]{:S(2)}) collective-permute-start(f32[2,16,8,1]{3,2,1,0:T(8,128)S(1)} %get-tuple-element.175), channel_id=1, source_target_pairs={{0,16},{16,32},{32,48},{48,64},{64,80},{80,96},{96,112},{112,128},... | collective-permute-start | bytes 3080 | tf_op jit(solution)/shard_map/ppermute | solution.py:16
  18.9 66.5 %collective-permute-start.5 = (f32[2,16,8,1]{3,2,1,0:T(8,128)S(1)}, f32[2,16,8,1]{3,2,1,0:T(8,128)S(1)}, u32[]{:S(2)}, u32[]{:S(2)}) collective-permute-start(f32[2,16,8,1]{3,2,1,0:T(8,128)S(1)} %get-tuple-element.176), channel_id=1, source_target_pairs={{16,0},{32,16},{48,32},{64,48},{80,64},{96,80},{112,96},{128,112},... | collective-permute-start | bytes 3080 | tf_op jit(solution)/shard_map/ppermute | solution.py:18
  31.9 11.9 %copy-start.9 = (s32[1,2048]{1,0:T(1,128)S(1)}, s32[1,2048]{1,0:T(1,128)}, u32[]{:S(2)}) copy-start(s32[1,2048]{1,0:T(1,128)} %param.20) | copy-start | bytes 24580
  31.9 11.9 %copy-start.8 = (s32[1,2048]{1,0:T(1,128)S(1)}, s32[1,2048]{1,0:T(1,128)}, u32[]{:S(2)}) copy-start(s32[1,2048]{1,0:T(1,128)} %param.21) | copy-start | bytes 24580
  31.9 53.6 %copy-start.1 = (f32[16,8,128]{2,1,0:T(8,128)S(1)}, f32[16,8,128]{2,1,0:T(8,128)}, u32[]{:S(2)}) copy-start(f32[16,8,128]{2,1,0:T(8,128)} %param.13) | copy-start | bytes 196612
  31.9 53.6 %copy-start.2 = (f32[16,8,128]{2,1,0:T(8,128)S(1)}, f32[16,8,128]{2,1,0:T(8,128)}, u32[]{:S(2)}) copy-start(f32[16,8,128]{2,1,0:T(8,128)} %param.12) | copy-start | bytes 196612
  31.9 61.8 %copy-start.3 = (f32[16,8,128]{2,1,0:T(8,128)S(1)}, f32[16,8,128]{2,1,0:T(8,128)}, u32[]{:S(2)}) copy-start(f32[16,8,128]{2,1,0:T(8,128)} %param.15) | copy-start | bytes 196612
  31.9 61.8 %copy-start.4 = (f32[16,8,128]{2,1,0:T(8,128)S(1)}, f32[16,8,128]{2,1,0:T(8,128)}, u32[]{:S(2)}) copy-start(f32[16,8,128]{2,1,0:T(8,128)} %param.14) | copy-start | bytes 196612
  31.9 61.8 %copy-start.6 = (f32[8,128]{1,0:T(8,128)S(1)}, f32[8,128]{1,0:T(8,128)}, u32[]{:S(2)}) copy-start(f32[8,128]{1,0:T(8,128)} %param.16) | copy-start | bytes 12292
  43.7 60.9 %copy-start.7 = (f32[15,8,128]{2,1,0:T(8,128)S(1)}, f32[15,8,128]{2,1,0:T(8,128)}, u32[]{:S(2)}) copy-start(f32[15,8,128]{2,1,0:T(8,128)} %param.17) | copy-start | bytes 184324
  85.7 16.3 %collective-permute-start.6 = (f32[2,16,1,130]{3,2,1,0:T(1,128)S(1)}, f32[2,16,1,130]{3,2,1,0:T(1,128)S(1)}, u32[]{:S(2)}, u32[]{:S(2)}) collective-permute-start(f32[2,16,1,130]{3,2,1,0:T(1,128)S(1)} %get-tuple-element.145), channel_id=1, source_target_pairs={{0,1},{1,2},{2,3},{3,4},{4,5},{5,6},{6,7},{7,8},{8,9},{9,10},{10,1... | collective-permute-start | bytes 49928 | tf_op jit(solution)/shard_map/ppermute | solution.py:16
  89.2 12.9 %collective-permute-start.7 = (f32[2,16,1,130]{3,2,1,0:T(1,128)S(1)}, f32[2,16,1,130]{3,2,1,0:T(1,128)S(1)}, u32[]{:S(2)}, u32[]{:S(2)}) collective-permute-start(f32[2,16,1,130]{3,2,1,0:T(1,128)S(1)} %get-tuple-element.146), channel_id=1, source_target_pairs={{1,0},{2,1},{3,2},{4,3},{5,4},{6,5},{7,6},{8,7},{9,8},{10,9},{11,1... | collective-permute-start | bytes 49928 | tf_op jit(solution)/shard_map/ppermute | solution.py:18
  94.1 8.3 %collective-permute-start.2 = (f32[34,2,132]{2,1,0:T(2,128)S(1)}, f32[34,2,132]{2,1,0:T(2,128)S(1)}, u32[]{:S(2)}, u32[]{:S(2)}) collective-permute-start(f32[34,2,132]{2,1,0:T(2,128)S(1)} %get-tuple-element.137), channel_id=1, source_target_pairs={{0,1},{1,2},{2,3},{3,4},{4,5},{5,6},{6,7},{7,8},{8,9},{9,10},{10,1... | collective-permute-start | bytes 107720 | tf_op jit(solution)/shard_map/ppermute | solution.py:16
  96.0 8.0 %collective-permute-start.3 = (f32[34,2,132]{2,1,0:T(2,128)S(1)}, f32[34,2,132]{2,1,0:T(2,128)S(1)}, u32[]{:S(2)}, u32[]{:S(2)}) collective-permute-start(f32[34,2,132]{2,1,0:T(2,128)S(1)} %get-tuple-element.138), channel_id=1, source_target_pairs={{1,0},{2,1},{3,2},{4,3},{5,4},{6,5},{7,6},{8,7},{9,8},{10,9},{11,1... | collective-permute-start | bytes 107720 | tf_op jit(solution)/shard_map/ppermute | solution.py:18
  106.7 11.6 %collective-permute-start.8 = (f32[2,16,8,1]{3,2,1,0:T(8,128)S(1)}, f32[2,16,8,1]{3,2,1,0:T(8,128)S(1)}, u32[]{:S(2)}, u32[]{:S(2)}) collective-permute-start(f32[2,16,8,1]{3,2,1,0:T(8,128)S(1)} %get-tuple-element.173), channel_id=1, source_target_pairs={{0,16},{16,32},{32,48},{48,64},{64,80},{80,96},{96,112},{112,128},... | collective-permute-start | bytes 3080 | tf_op jit(solution)/shard_map/ppermute | solution.py:16
  106.8 11.6 %collective-permute-start.9 = (f32[2,16,8,1]{3,2,1,0:T(8,128)S(1)}, f32[2,16,8,1]{3,2,1,0:T(8,128)S(1)}, u32[]{:S(2)}, u32[]{:S(2)}) collective-permute-start(f32[2,16,8,1]{3,2,1,0:T(8,128)S(1)} %get-tuple-element.174), channel_id=1, source_target_pairs={{16,0},{32,16},{48,32},{64,48},{80,64},{96,80},{112,96},{128,112},... | collective-permute-start | bytes 3080 | tf_op jit(solution)/shard_map/ppermute | solution.py:18
  109.7 8.6 %copy-start.5 = (s32[1,2048]{1,0:T(1,128)S(1)}, s32[1,2048]{1,0:T(1,128)}, u32[]{:S(2)}) copy-start(s32[1,2048]{1,0:T(1,128)} %param.19) | copy-start | bytes 24580
  118.7 8.3 %collective-permute-start.10 = (f32[2,16,1,130]{3,2,1,0:T(1,128)S(1)}, f32[2,16,1,130]{3,2,1,0:T(1,128)S(1)}, u32[]{:S(2)}, u32[]{:S(2)}) collective-permute-start(f32[2,16,1,130]{3,2,1,0:T(1,128)S(1)} %get-tuple-element.143), channel_id=1, source_target_pairs={{0,1},{1,2},{2,3},{3,4},{4,5},{5,6},{6,7},{7,8},{8,9},{9,10},{10,1... | collective-permute-start | bytes 49928 | tf_op jit(solution)/shard_map/ppermute | solution.py:16
  120.6 8.0 %collective-permute-start.11 = (f32[2,16,1,130]{3,2,1,0:T(1,128)S(1)}, f32[2,16,1,130]{3,2,1,0:T(1,128)S(1)}, u32[]{:S(2)}, u32[]{:S(2)}) collective-permute-start(f32[2,16,1,130]{3,2,1,0:T(1,128)S(1)} %get-tuple-element.144), channel_id=1, source_target_pairs={{1,0},{2,1},{3,2},{4,3},{5,4},{6,5},{7,6},{8,7},{9,8},{10,9},{11,1... | collective-permute-start | bytes 49928 | tf_op jit(solution)/shard_map/ppermute | solution.py:18
  130.0 5.6 %collective-permute-start.12 = (f32[2,16,8,1]{3,2,1,0:T(8,128)S(1)}, f32[2,16,8,1]{3,2,1,0:T(8,128)S(1)}, u32[]{:S(2)}, u32[]{:S(2)}) collective-permute-start(f32[2,16,8,1]{3,2,1,0:T(8,128)S(1)} %get-tuple-element.171), channel_id=1, source_target_pairs={{0,16},{16,32},{32,48},{48,64},{64,80},{80,96},{96,112},{112,128},... | collective-permute-start | bytes 3080 | tf_op jit(solution)/shard_map/ppermute | solution.py:16
  130.0 5.6 %collective-permute-start.13 = (f32[2,16,8,1]{3,2,1,0:T(8,128)S(1)}, f32[2,16,8,1]{3,2,1,0:T(8,128)S(1)}, u32[]{:S(2)}, u32[]{:S(2)}) collective-permute-start(f32[2,16,8,1]{3,2,1,0:T(8,128)S(1)} %get-tuple-element.172), channel_id=1, source_target_pairs={{16,0},{32,16},{48,32},{64,48},{80,64},{96,80},{112,96},{128,112},... | collective-permute-start | bytes 3080 | tf_op jit(solution)/shard_map/ppermute | solution.py:18
  135.9 8.3 %collective-permute-start.14 = (f32[2,16,1,130]{3,2,1,0:T(1,128)S(1)}, f32[2,16,1,130]{3,2,1,0:T(1,128)S(1)}, u32[]{:S(2)}, u32[]{:S(2)}) collective-permute-start(f32[2,16,1,130]{3,2,1,0:T(1,128)S(1)} %get-tuple-element.141), channel_id=1, source_target_pairs={{0,1},{1,2},{2,3},{3,4},{4,5},{5,6},{6,7},{7,8},{8,9},{9,10},{10,1... | collective-permute-start | bytes 49928 | tf_op jit(solution)/shard_map/ppermute | solution.py:16
  140.7 5.8 %collective-permute-start.15 = (f32[2,16,1,130]{3,2,1,0:T(1,128)S(1)}, f32[2,16,1,130]{3,2,1,0:T(1,128)S(1)}, u32[]{:S(2)}, u32[]{:S(2)}) collective-permute-start(f32[2,16,1,130]{3,2,1,0:T(1,128)S(1)} %get-tuple-element.142), channel_id=1, source_target_pairs={{1,0},{2,1},{3,2},{4,3},{5,4},{6,5},{7,6},{8,7},{9,8},{10,9},{11,1... | collective-permute-start | bytes 49928 | tf_op jit(solution)/shard_map/ppermute | solution.py:18
  147.9 5.6 %collective-permute-start.16 = (f32[2,16,8,1]{3,2,1,0:T(8,128)S(1)}, f32[2,16,8,1]{3,2,1,0:T(8,128)S(1)}, u32[]{:S(2)}, u32[]{:S(2)}) collective-permute-start(f32[2,16,8,1]{3,2,1,0:T(8,128)S(1)} %get-tuple-element.169), channel_id=1, source_target_pairs={{0,16},{16,32},{32,48},{48,64},{64,80},{80,96},{96,112},{112,128},... | collective-permute-start | bytes 3080 | tf_op jit(solution)/shard_map/ppermute | solution.py:16
  147.9 5.6 %collective-permute-start.17 = (f32[2,16,8,1]{3,2,1,0:T(8,128)S(1)}, f32[2,16,8,1]{3,2,1,0:T(8,128)S(1)}, u32[]{:S(2)}, u32[]{:S(2)}) collective-permute-start(f32[2,16,8,1]{3,2,1,0:T(8,128)S(1)} %get-tuple-element.170), channel_id=1, source_target_pairs={{16,0},{32,16},{48,32},{64,48},{80,64},{96,80},{112,96},{128,112},... | collective-permute-start | bytes 3080 | tf_op jit(solution)/shard_map/ppermute | solution.py:18
  153.8 8.2 %collective-permute-start.18 = (f32[2,16,1,130]{3,2,1,0:T(1,128)S(1)}, f32[2,16,1,130]{3,2,1,0:T(1,128)S(1)}, u32[]{:S(2)}, u32[]{:S(2)}) collective-permute-start(f32[2,16,1,130]{3,2,1,0:T(1,128)S(1)} %get-tuple-element.139), channel_id=1, source_target_pairs={{0,1},{1,2},{2,3},{3,4},{4,5},{5,6},{6,7},{7,8},{8,9},{9,10},{10,1... | collective-permute-start | bytes 49928 | tf_op jit(solution)/shard_map/ppermute | solution.py:16
  159.0 5.8 %collective-permute-start.19 = (f32[2,16,1,130]{3,2,1,0:T(1,128)S(1)}, f32[2,16,1,130]{3,2,1,0:T(1,128)S(1)}, u32[]{:S(2)}, u32[]{:S(2)}) collective-permute-start(f32[2,16,1,130]{3,2,1,0:T(1,128)S(1)} %get-tuple-element.140), channel_id=1, source_target_pairs={{1,0},{2,1},{3,2},{4,3},{5,4},{6,5},{7,6},{8,7},{9,8},{10,9},{11,1... | collective-permute-start | bytes 49928 | tf_op jit(solution)/shard_map/ppermute | solution.py:18
Sparse Core Ops, SparseCore 0:
  186.6 115.9 reduce-scatter.1
where the time goes:
time: 313 us; the launch traced here: 311 us
  waiting for transfers between devices  129 us (41%)
  other arithmetic  73.7 us (24%)
  starting transfers between devices  61.4 us (20%)
  local copies, waits for them, and re-layouts  31.8 us (10%)
  between operations  14.9 us (5%)
    reduce_scatter x1, waiting for transfers between devices, shards(): lax.psum_scatter(partial_sums, 'gx', scatter_dimension=1, tiled=True)  115 us
    ppermute x10, starting transfers between devices, with_halo(): lax.ppermute(head, axis, [((i + 1) % count, i) for i in range(count)])  44 us
    gather x3, other arithmetic, shards(): jnp.take(patch_measures, patch_measure_pointer[0])  41.6 us
    scatter-add x1, other arithmetic, shards(): jnp.zeros((2, row_cells), jnp.float32).at[:, places].add(terms)  19.5 us
    ppermute x10, starting transfers between devices, with_halo(): lax.ppermute(tail, axis, [(i, (i + 1) % count) for i in range(count)])  17.4 us
    gather x1, local copies, waits for them, and re-layouts, shards(): places = jnp.take(holder_ordering[0], patch_sky_target[0])  11.8 us
    gather x1, local copies, waits for them, and re-layouts, shards(): jnp.take(wet_top, cells)  8.58 us
    ppermute x10, waiting for transfers between devices, with_halo(): lax.ppermute(head, axis, [((i + 1) % count, i) for i in range(count)])  8.34 us
  transfers between devices with their start and end apart: 21, of which 7 were waited for; matrix products, arithmetic and copies ran while one was open for 24% of the time, Pallas kernels for 0%

commit v1 on v0

v1 whole, which is shorter than its diff:
```python
import jax
import jax.numpy as jnp
from jax import lax
from jax.experimental import pallas as pl
from jax.experimental.pallas import tpu as pltpu
from jax.sharding import PartitionSpec as P

NSUB = 4
LEVELS = 16
ROWS = 8
LANES = 128
F32 = jnp.float32
BF16 = jnp.bfloat16


def iota(shape, dim):
    return lax.broadcasted_iota(jnp.int32, shape, dim)


def row_mask(parity):
    return (((iota((ROWS, LANES), 0) >> 2) + parity) & 1) == 0


def pack_kernel(t_ref, s_ref, u_ref, v_ref, kap_ref, dep_ref, col_ref, one_ref, two_ref):
    slot = iota((ROWS, LANES), 1) >> 3
    mask = row_mask(lax.axis_index("gy") & 1)
    for a, ref in enumerate((t_ref, s_ref, u_ref, v_ref)):
        strip = jnp.zeros((ROWS, LANES), F32)
        for k in range(LEVELS):
            strip = jnp.where(slot == k, pltpu.roll(ref[k], (8 * k + 4) % LANES, 1), strip)
        col_ref[a] = strip
        for k in range(8):
            here, there = ref[k], pltpu.roll(ref[k + 8], 4, 0)
            one_ref[a * 8 + k] = jnp.where(mask, there, here)
            two_ref[a * 8 + k] = jnp.where(mask, here, there)
    kap = kap_ref[...]
    dep = dep_ref[...].astype(F32)
    strip = jnp.where(slot == 0, pltpu.roll(kap, 4, 1), jnp.zeros((ROWS, LANES), F32))
    col_ref[4] = jnp.where(slot == 1, pltpu.roll(dep, 12, 1), strip)
    there = pltpu.roll(dep, 4, 0)
    one_ref[32] = jnp.where(mask, there, kap)
    two_ref[32] = jnp.where(mask, kap, there)


def side_columns(first_ref, second_ref):
    parity = lax.axis_index("gx") & 1
    mask = (((iota((ROWS, LANES), 1) >> 2) + parity) & 1) == 0
    return [jnp.where(mask, second_ref[a], first_ref[a]) for a in range(5)]


def corner_kernel(one_in, two_in, first_ref, second_ref, one_ref, two_ref):
    for i in range(33):
        one_ref[i] = one_in[i]
        two_ref[i] = two_in[i]
    side = side_columns(first_ref, second_ref)
    side.append(jnp.zeros((ROWS, LANES), F32))
    mask = row_mask(lax.axis_index("gy") & 1)
    for i in range(3):
        here, there = side[2 * i], pltpu.roll(side[2 * i + 1], 4, 0)
        one_ref[33 + i] = jnp.where(mask, there, here)
        two_ref[33 + i] = jnp.where(mask, here, there)


def prep_kernel(
    src_ref, sky_ref, ptr_ref, area_ref, place_ref, mix_ref, dep_ref,
    inv_ref, down_ref, up_ref, weight_ref, owner_ref, rank_ref, slot_ref,
):
    q = lax.axis_index("gx")
    dep = dep_ref[...]
    above = jnp.zeros((ROWS, LANES), F32)
    carry = jnp.zeros((ROWS, LANES), F32)
    for k in range(LEVELS):
        below = jnp.where(dep > k + 1, mix_ref[k], 0.0) if k < LEVELS - 1 else jnp.zeros((ROWS, LANES), F32)
        inv = 1.0 / ((1.0 + above + below) - above * carry)
        carry = below * inv
        inv_ref[k] = inv
        down_ref[k] = above * inv
        up_ref[k] = carry
        above = below
    src = src_ref[...]
    sky = sky_ref[...]
    row, col = src >> 7, src & 127
    table = area_ref[...]
    table = jnp.broadcast_to(jnp.concatenate([table, table], axis=1), (16, LANES))
    area = jnp.take_along_axis(table, ptr_ref[...], axis=1)
    rise = (sky >> 11) - (row >> 1)
    east = ((sky & 2047) - (q * 64 + (col >> 1))) & 2047
    kind = jnp.where(east == 1, 1, jnp.where(rise == 1, 2, jnp.where(rise == -1, 3, 0)))
    high = kind * 8 + row
    part = []
    rest = area
    for _ in range(3):
        piece = rest.astype(BF16).astype(F32)
        part.append(piece)
        rest = rest - piece
    sums = jnp.zeros((96, LANES), F32)
    for i in range(0, 16, 2):
        left, right = [], []
        for j in (i, i + 1):
            hit = jnp.broadcast_to(high[j : j + 1], (32, LANES)) == iota((32, LANES), 0)
            left.append(
                jnp.concatenate(
                    [jnp.where(hit, jnp.broadcast_to(p[j : j + 1], (32, LANES)), 0.0) for p in part], axis=0
                )
            )
            same = jnp.broadcast_to(col[j : j + 1], (LANES, LANES)) == iota((LANES, LANES), 0)
            right.append(jnp.where(same, 1.0, 0.0))
        sums = sums + lax.dot_general(
            jnp.concatenate(left, axis=1).astype(BF16),
            jnp.concatenate(right, axis=1).astype(BF16),
            (((1,), (1,)), ((), ())),
            preferred_element_type=F32,
        )
    sums = sums[0:32] + sums[32:64] + sums[64:96]
    wet = jnp.where(dep > 0, 1.0, 0.0)
    for m in range(4):
        weight_ref[m] = sums[m * 8 : m * 8 + 8] * wet
    lane = iota((ROWS, LANES), 1)
    sub = iota((ROWS, LANES), 0)
    nextq = (q + 1) & 31
    own, hot = [], []
    outside = jnp.full((ROWS, LANES), -1, jnp.int32)
    for r in range(4):
        line = jnp.broadcast_to(place_ref[pl.ds(r * 16 + (q >> 1), 1), :], (ROWS, LANES))
        place = jnp.take_along_axis(line, (lane >> 1) + 64 * (q & 1), axis=1)
        own.append(place)
        hot.append(jnp.where(jnp.broadcast_to(place[0:1] >> 8, (32, LANES)) == iota((32, LANES), 0), 1.0, 0.0))
        line = jnp.broadcast_to(place_ref[pl.ds(r * 16 + (nextq >> 1), 1), :], (ROWS, LANES))
        place = jnp.take_along_axis(line, (lane & 0) + 64 * (nextq & 1), axis=1)
        outside = jnp.where((lane >> 1) == r, place, outside)
    hot.append(jnp.where(jnp.broadcast_to(outside[0:1] >> 8, (32, LANES)) == iota((32, LANES), 0), 1.0, 0.0))
    owner = jnp.concatenate(hot, axis=1).astype(BF16)
    owner_ref[...] = owner
    stacked = jnp.concatenate(hot[:4], axis=0).astype(BF16)
    low, this = iota((LANES, LANES), 0), iota((LANES, LANES), 1)
    single = (low & 1) == 0
    before = jnp.where(single & ((low >> 1) < (this >> 1)), 1.0, 0.0).astype(BF16)
    every = jnp.where(single, 1.0, 0.0).astype(BF16)
    ahead = jnp.dot(stacked, before, preferred_element_type=F32)
    whole = jnp.dot(stacked, every, preferred_element_type=F32)
    carried = jnp.zeros((32, LANES), F32)
    slots = []
    for r in range(4):
        count = ahead[r * 32 : r * 32 + 32] + carried
        carried = carried + whole[r * 32 : r * 32 + 32]
        rank = jnp.sum(hot[r] * count, axis=0, keepdims=True).astype(jnp.int32)
        chosen = jnp.where(jnp.broadcast_to(rank, (ROWS, LANES)) == sub, 1.0, 0.0)
        rank_ref[r] = chosen
        slots.append(jnp.where((lane & 1) == 0, chosen * (own[r] & 255).astype(F32), 0.0))
    slots.append(jnp.zeros((ROWS, LANES), F32))
    main = jnp.concatenate(slots, axis=1)
    extra = jnp.where(lane == 2 * sub, (outside & 255).astype(F32), 0.0)
    extra = jnp.where(sub < 4, extra, 0.0)
    extra = jnp.concatenate([jnp.zeros((ROWS, 4 * LANES), F32), extra], axis=1)
    lines = jnp.concatenate(
        [jnp.zeros((24, 5 * LANES), F32), main, extra, jnp.zeros((88, 5 * LANES), F32)], axis=0
    ).astype(BF16)
    slot_ref[...] = lax.dot_general(owner, lines, (((1,), (1,)), ((), ())), preferred_element_type=F32)


def main_kernel(
    t_ref, s_ref, u_ref, v_ref, kap_ref, dep_ref, first_ref, second_ref, one_ref, two_ref,
    inv_ref, down_ref, up_ref, weight_ref, owner_ref, rank_ref, slot_ref,
    tout_ref, sout_ref, send_ref,
):
    shape = (ROWS, LANES)
    lane, sub = iota(shape, 1), iota(shape, 0)
    lane_first, lane_last = lane == 0, lane == LANES - 1
    row_first, row_last = sub == 0, sub == ROWS - 1
    mask = row_mask(lax.axis_index("gy") & 1)

    def ring(x, y, shift, axis, edge):
        rx, ry = pltpu.roll(x, shift, axis), pltpu.roll(y, shift, axis)
        return jnp.where(edge, ry, rx), jnp.where(edge, rx, ry)

    def east(f):
        a, b = ring(f[0], f[1], LANES - 1, 1, lane_last)
        h, g = ring(f[2], f[3], LANES - 1, 1, lane_last)
        return a, b, h, g

    def west(f):
        a, b = ring(f[0], f[1], 1, 1, lane_first)
        h, g = ring(f[2], f[3], 1, 1, lane_first)
        return a, b, h, g

    def north(f):
        a, h = ring(f[0], f[2], ROWS - 1, 0, row_last)
        b, g = ring(f[1], f[3], ROWS - 1, 0, row_last)
        return a, b, h, g

    def south(f):
        a, h = ring(f[0], f[2], 1, 0, row_first)
        b, g = ring(f[1], f[3], 1, 0, row_first)
        return a, b, h, g

    def pair(i):
        x, y = one_ref[i], two_ref[i]
        return jnp.where(mask, x, y), pltpu.roll(jnp.where(mask, y, x), 4, 0)

    side = side_columns(first_ref, second_ref)
    corner = []
    for i in range(3):
        corner.extend(pair(33 + i))

    def field(local, plane, k, outer):
        shift = (LANES - 8 * k - 4) % LANES
        return local, pltpu.roll(side[plane], shift, 1), outer, pltpu.roll(corner[plane], shift, 1)

    outer_kap, outer_dep = pair(32)
    kap = field(kap_ref[...], 4, 0, outer_kap)
    dep = field(dep_ref[...].astype(F32), 4, 1, outer_dep)
    kap_east = [0.5 * (x + y) for x, y in zip(kap, east(kap))]
    kap_north = [0.5 * (x + y) for x, y in zip(kap, north(kap))]
    dep_east = [jnp.minimum(x, y) for x, y in zip(dep, east(dep))]
    dep_north = [jnp.minimum(x, y) for x, y in zip(dep, north(dep))]

    def level(k, outer):
        u = field(u_ref[k], 2, k, outer[2])
        v = field(v_ref[k], 3, k, outer[3])
        level_f = float(k)

        def face(rate, kappa, depth):
            here = [
                jnp.where(d > level_f, jnp.maximum(r, 0.0) + c, 0.0) for r, c, d in zip(rate, kappa, depth)
            ]
            there = [
                jnp.where(d > level_f, c - jnp.minimum(r, 0.0), 0.0) for r, c, d in zip(rate, kappa, depth)
            ]
            return here, there

        here_e, from_e = face(u, kap_east, dep_east)
        here_n, from_n = face(v, kap_north, dep_north)
        from_w = west(here_e)
        from_s = south(here_n)
        back_e = west(from_e)
        back_n = south(from_n)
        keep = [
            1.0 - ((a + b) + (c + d)) for a, b, c, d in zip(here_e, back_e, here_n, back_n)
        ]
        for which, (in_ref, out_ref) in enumerate(((t_ref, tout_ref), (s_ref, sout_ref))):
            c = field(in_ref[k], which, k, outer[which])
            for step in range(NSUB):
                around = zip(keep, c, from_e, east(c), from_w, west(c), from_n, north(c), from_s, south(c))
                new = []
                for c0, x, ce, xe, cw, xw, cn, xn, cs, xs in around:
                    new.append((c0 * x + (ce * xe + cw * xw)) + (cn * xn + cs * xs))
                    if step == NSUB - 1:
                        break
                c = new
            out_ref[k] = c[0]

    for k in range(8):
        pairs = [pair(a * 8 + k) for a in range(4)]
        level(k, [p[0] for p in pairs])
        level(k + 8, [p[1] for p in pairs])

    tops = []
    for out_ref in (tout_ref, sout_ref):
        value = out_ref[0] * inv_ref[0]
        values = [value]
        for k in range(1, LEVELS):
            value = out_ref[k] * inv_ref[k] + down_ref[k] * value
            values.append(value)
        out_ref[LEVELS - 1] = value
        for k in range(LEVELS - 2, -1, -1):
            value = values[k] + up_ref[k] * value
            out_ref[k] = value
        tops.append(value)

    lines, extra = [], jnp.zeros(shape, F32)
    for t, top in enumerate(tops):
        moved = pltpu.roll(weight_ref[1] * top, 2, 1)
        beyond = lane < 2
        total = weight_ref[0] * top + jnp.where(beyond, 0.0, moved)
        total = total + pltpu.roll(weight_ref[2] * top, 2, 0)
        total = total + pltpu.roll(weight_ref[3] * top, ROWS - 2, 0)
        total = total + pltpu.roll(total, ROWS - 1, 0)
        moved = jnp.where(beyond, moved, 0.0)
        moved = moved + pltpu.roll(moved, ROWS - 1, 0)
        blocks = []
        for r in range(4):
            blocks.append(rank_ref[r] * jnp.broadcast_to(total[2 * r : 2 * r + 1], shape))
            line = jnp.broadcast_to(moved[2 * r : 2 * r + 1], shape)
            line = pltpu.roll(line, 2 * r, 1) if r else line
            extra = jnp.where(sub == 4 * t + r, line, extra)
        blocks.append(jnp.zeros(shape, F32))
        lines.append(jnp.concatenate(blocks, axis=1))
    lines.append(jnp.concatenate([jnp.zeros((ROWS, 4 * LANES), F32), extra], axis=1))
    rest = jnp.concatenate(lines, axis=0)
    owner = owner_ref[...]
    send = jnp.zeros((32, 24), F32)
    for _ in range(3):
        piece = rest.astype(BF16)
        rest = rest - piece.astype(F32)
        send = send + lax.dot_general(owner, piece, (((1,), (1,)), ((), ())), preferred_element_type=F32)
    send_ref[...] = slot_ref[...]
    send_ref[:, 0:24] = send


def owner_kernel(got_ref, air_ref):
    got = got_ref[...]
    shape = (32, LANES)
    lane = iota(shape, 1).astype(F32)
    sums = [[jnp.zeros(shape, F32) for _ in range(2)] for _ in range(2)]
    for j in range(12):
        first, second, place = (j, 8 + j, 24 + j) if j < 8 else (8 + j, 12 + j, 24 + j)
        slot = jnp.broadcast_to(got[:, place : place + 1], shape)
        terms = [jnp.broadcast_to(got[:, first : first + 1], shape), jnp.broadcast_to(got[:, second : second + 1], shape)]
        for half in range(2):
            hit = slot == lane + float(half * LANES)
            for t in range(2):
                sums[t][half] = sums[t][half] + jnp.where(hit, terms[t], 0.0)
    for t in range(2):
        for half in range(2):
            air_ref[t, :, half * LANES : half * LANES + LANES] = jnp.sum(sums[t][half], axis=0, keepdims=True)


VMEM = pl.BlockSpec(memory_space=pltpu.VMEM)


def call(kernel, name, outs, n_in, flops, **kw):
    return pl.pallas_call(
        kernel,
        name=name,
        out_shape=tuple(jax.ShapeDtypeStruct(s, d) for s, d in outs),
        in_specs=[VMEM] * n_in,
        out_specs=tuple([VMEM] * len(outs)),
        cost_estimate=pl.CostEstimate(flops=flops, bytes_accessed=1 << 20, transcendentals=0),
        compiler_params=pltpu.CompilerParams(vmem_limit_bytes=16 << 20),
        **kw,
    )


def shards(
    thermal_anomaly,
    saltiness_anomaly,
    zonal_volume_rate,
    meridional_volume_rate,
    sideways_diffusivity_factor,
    stratum_interface_mixing,
    flooded_strata,
    patch_sea_source,
    patch_sky_target,
    patch_measure_pointer,
    patch_measures,
    holder_ordering,
):
    nx, ny = lax.axis_size("gx"), lax.axis_size("gy")
    fields = (
        thermal_anomaly,
        saltiness_anomaly,
        zonal_volume_rate,
        meridional_volume_rate,
        sideways_diffusivity_factor,
        flooded_strata,
    )
    plane = (ROWS, LANES)
    strips = ((36,) + plane, F32)
    column, one, two = call(pack_kernel, "pack", [((5,) + plane, F32), strips, strips], 6, 1 << 20)(*fields)

    def swap(x, axis, count, start, wrap):
        pairs = []
        for i in range(start, count, 2):
            if i + 1 < count or wrap:
                pairs += [(i, (i + 1) % count), ((i + 1) % count, i)]
        return lax.ppermute(x, axis, pairs)

    first = swap(column, "gx", nx, 0, True)
    second = swap(column, "gx", nx, 1, True)
    one, two = call(corner_kernel, "corner", [strips, strips], 4, 1 << 16)(
        one, two, first, second
    )
    one = swap(one, "gy", ny, 0, False)
    two = swap(two, "gy", ny, 1, False)
    column3 = ((LEVELS,) + plane, F32)
    prepared = call(
        prep_kernel,
        "prep",
        [
            column3,
            column3,
            column3,
            ((4,) + plane, F32),
            ((32, 5 * LANES), BF16),
            ((4,) + plane, F32),
            ((32, LANES), F32),
        ],
        7,
        1 << 26,
    )(
        patch_sea_source.reshape(16, LANES),
        patch_sky_target.reshape(16, LANES),
        patch_measure_pointer.reshape(16, LANES),
        patch_measures.reshape(1, 64),
        holder_ordering.reshape(64, LANES),
        stratum_interface_mixing,
        flooded_strata,
    )
    temperature, salinity, send = call(
        main_kernel, "main", [column3, column3, ((32, LANES), F32)], 17, 1 << 24
    )(*fields, first, second, one, two, *prepared)
    got = lax.all_to_all(send.reshape(nx, 1, LANES), "gx", 0, 0, tiled=True)
    (air,) = call(owner_kernel, "owner", [((2, 1, 256), F32)], 1, 1 << 20)(got.reshape(nx, LANES))
    return temperature, salinity, air


def solution(mesh):
    placed = (
        P(None, "gy", "gx"),
        P(None, "gy", "gx"),
        P(None, "gy", "gx"),
        P(None, "gy", "gx"),
        P("gy", "gx"),
        P(None, "gy", "gx"),
        P("gy", "gx"),
        P("gy", "gx"),
        P("gy", "gx"),
        P("gy", "gx"),
        P(),
        P("gy", None),
    )
    return jax.shard_map(
        shards,
        mesh=mesh,
        in_specs=placed,
        out_specs=(P(None, "gy", "gx"), P(None, "gy", "gx"), P(None, "gy", "gx")),
        check_vma=False,
    )
```

time: 313 us -> 61.3 us (0.20)
  waiting for transfers between devices: 129 us -> 5.75 us
  other arithmetic: 73.7 us -> 0 us
  starting transfers between devices: 61.4 us -> 21.1 us
  local copies, waits for them, and re-layouts: 31.8 us -> 4.77 us
  blocking collectives: 0 us -> 21.1 us
  between operations: 14.9 us -> 0.82 us
  Pallas kernels: 0 us -> 7.28 us
    reduce_scatter x1 -> x0, waiting for transfers between devices: 115 us -> none  [shards(): lax.psum_scatter(partial_sums, 'gx', scatter_dimension=1, tiled=True)]
    gather x4 -> x0, other arithmetic: 41.6 us -> none  [the longest x3 41.6 us: shards(): jnp.take(patch_measures, patch_measure_pointer[0])]
    ppermute x20 -> x4, starting transfers between devices: 61.4 us -> 21.1 us  [swap(): return lax.ppermute(x, axis, pairs)]
    gather x6 -> x0, local copies, waits for them, and re-layouts: 28.2 us -> none  [the longest x1 11.8 us: shards(): places = jnp.take(holder_ordering[0], patch_sky_target[0])]
    all_to_all x0 -> x1, blocking collectives: none -> 21.1 us  [shards(): got = lax.all_to_all(send.reshape(nx, 1, LANES), 'gx', 0, 0, tiled=True)]
    scatter-add x1 -> x0, other arithmetic: 19.5 us -> none  [shards(): jnp.zeros((2, row_cells), jnp.float32).at[:, places].add(terms)]
    ppermute x20 -> x4, waiting for transfers between devices: 13.7 us -> 5.75 us  [swap(): return lax.ppermute(x, axis, pairs)]
    pallas_call x0 -> x5, Pallas kernels: none -> 7.28 us  [the longest x1 5.72 us: shards(): call(main_kernel, 'main', [column3, column3, ((32, LANES), F32)], 17, 1 <...]
  transfers between devices with their start and end apart: 21 -> 4, of which waited for: 7 -> 2; matrix products, arithmetic and copies ran while one was open for 24% -> 0% of each run, Pallas kernels for 0% -> 1%
where the time goes in v1:
time: 61.3 us; the launch traced here: 60.8 us
  starting transfers between devices  21.1 us (34%)
  blocking collectives  21.1 us (34%)
  Pallas kernels  7.28 us (12%)
  waiting for transfers between devices  5.75 us (9%)
  local copies, waits for them, and re-layouts  4.77 us (8%)
  between operations  0.82 us (1%)
    ppermute x4, starting transfers between devices, swap(): return lax.ppermute(x, axis, pairs)  21.1 us
    all_to_all x1, blocking collectives, shards(): got = lax.all_to_all(send.reshape(nx, 1, LANES), 'gx', 0, 0, tiled=True)  21.1 us
    ppermute x4, waiting for transfers between devices, swap(): return lax.ppermute(x, axis, pairs)  5.75 us
    pallas_call x1, Pallas kernels, shards(): call(main_kernel, 'main', [column3, column3, ((32, LANES), F32)], 17, 1 <...  5.72 us
    unnamed x32, local copies, waits for them, and re-layouts  4.77 us
  transfers between devices with their start and end apart: 4, of which 2 were waited for; matrix products, arithmetic and copies ran while one was open for 0% of the time, Pallas kernels for 1%

profile of v1, /device:TPU:24, one launch (start us, length us, event | category | flops | bytes accessed | tf_op | source)
XLA Modules:
  0.0 60.8 jit_solution(17739790312217225824)
XLA Ops:
  0.6 0.0 copy-start
  0.6 0.8 %copy-done = f32[16,8,128]{2,1,0:T(8,128)S(1)} copy-done((f32[16,8,128]{2,1,0:T(8,128)S(1)}, f32[16,8,128]{2,1,0:T(8,128)}, u32[]{:S(2)}) %copy-start) | copy-done | bytes 65560
  1.5 0.0 copy-start.2
  1.5 0.8 %copy-done.2 = f32[16,8,128]{2,1,0:T(8,128)S(1)} copy-done((f32[16,8,128]{2,1,0:T(8,128)S(1)}, f32[16,8,128]{2,1,0:T(8,128)}, u32[]{:S(2)}) %copy-start.2) | copy-done | bytes 65560
  2.3 0.0 copy-start.4
  2.3 0.8 %copy-done.4 = f32[16,8,128]{2,1,0:T(8,128)S(1)} copy-done((f32[16,8,128]{2,1,0:T(8,128)S(1)}, f32[16,8,128]{2,1,0:T(8,128)}, u32[]{:S(2)}) %copy-start.4) | copy-done | bytes 65560
  3.2 0.0 copy-start.6
  3.2 0.8 %copy-done.6 = f32[16,8,128]{2,1,0:T(8,128)S(1)} copy-done((f32[16,8,128]{2,1,0:T(8,128)S(1)}, f32[16,8,128]{2,1,0:T(8,128)}, u32[]{:S(2)}) %copy-start.6) | copy-done | bytes 65560
  4.0 0.0 copy-start.8
  4.0 0.7 %copy-done.8 = f32[8,128]{1,0:T(8,128)S(1)} copy-done((f32[8,128]{1,0:T(8,128)S(1)}, f32[8,128]{1,0:T(8,128)}, u32[]{:S(2)}) %copy-start.8) | copy-done | bytes 4120
  4.7 0.0 copy-start.9
  4.7 0.7 %copy-done.9 = s32[8,128]{1,0:T(8,128)S(1)} copy-done((s32[8,128]{1,0:T(8,128)S(1)}, s32[8,128]{1,0:T(8,128)}, u32[]{:S(2)}) %copy-start.9) | copy-done | bytes 4120
  5.4 0.1 pack.1
  5.5 1.9 %collective-permute-start = (f32[5,8,128]{2,1,0:T(8,128)S(1)}, f32[5,8,128]{2,1,0:T(8,128)S(1)}, u32[]{:S(2)}, u32[]{:S(2)}) collective-permute-start(f32[5,8,128]{2,1,0:T(8,128)S(1)} %get-tuple-element.18), channel_id=1, source_target_pairs={{0,16},{16,0},{32,48},{48,32},{64,80},{80,64},{96,112},{112,96},{1... | collective-permute-start | bytes 61448 | tf_op jit(solution)/shard_map/ppermute | solution.py:366
  7.4 11.5 %collective-permute-start.1 = (f32[5,8,128]{2,1,0:T(8,128)S(1)}, f32[5,8,128]{2,1,0:T(8,128)S(1)}, u32[]{:S(2)}, u32[]{:S(2)}) collective-permute-start(f32[5,8,128]{2,1,0:T(8,128)S(1)} %get-tuple-element.18), channel_id=1, source_target_pairs={{16,32},{32,16},{48,64},{64,48},{80,96},{96,80},{112,128},{128,112... | collective-permute-start | bytes 61448 | tf_op jit(solution)/shard_map/ppermute | solution.py:366
  18.9 0.0 collective-permute-done.first_ref
  19.0 1.4 %collective-permute-done.1.second_ref = f32[5,8,128]{2,1,0:T(8,128)S(1)} collective-permute-done((f32[5,8,128]{2,1,0:T(8,128)S(1)}, f32[5,8,128]{2,1,0:T(8,128)S(1)}, u32[]{:S(2)}, u32[]{:S(2)}) %collective-permute-start.1) | collective-permute-done | bytes 20512 | tf_op jit(solution)/shard_map/ppermute | solution.py:366
  20.4 0.0 copy-start.10
  20.4 0.0 copy-start.11
  20.4 0.0 copy-start.13
  20.4 0.0 copy-start.14
  20.4 0.0 copy-start.15
  20.5 0.0 copy-start.12
  20.5 3.5 %collective-permute-start.2 = (f32[36,8,128]{2,1,0:T(8,128)S(1)}, f32[36,8,128]{2,1,0:T(8,128)S(1)}, u32[]{:S(2)}, u32[]{:S(2)}) collective-permute-start(f32[36,8,128]{2,1,0:T(8,128)S(1)} %get-tuple-element.21), channel_id=1, source_target_pairs={{0,1},{1,0},{2,3},{3,2},{4,5},{5,4},{6,7},{7,6},{8,9},{9,8},{10,11... | collective-permute-start | bytes 442376 | tf_op jit(solution)/shard_map/ppermute | solution.py:366
  24.0 4.2 %collective-permute-start.3 = (f32[36,8,128]{2,1,0:T(8,128)S(1)}, f32[36,8,128]{2,1,0:T(8,128)S(1)}, u32[]{:S(2)}, u32[]{:S(2)}) collective-permute-start(f32[36,8,128]{2,1,0:T(8,128)S(1)} %get-tuple-element.22), channel_id=1, source_target_pairs={{1,2},{2,1},{3,4},{4,3},{5,6},{6,5},{7,8},{8,7},{9,10},{10,9},{11,... | collective-permute-start | bytes 442376 | tf_op jit(solution)/shard_map/ppermute | solution.py:366
  28.2 0.0 copy-start.7
  28.2 0.0 copy-done.10
  28.2 0.0 copy-done.11
  28.2 0.0 copy-done.13
  28.2 0.0 copy-done.14
  28.3 0.0 copy-done.15
  28.3 0.0 copy-done.12
  28.3 0.0 copy-start.1
  28.3 0.0 copy-start.3
  28.3 0.0 copy-start.5
  28.3 0.5 prep.1
  28.8 0.0 collective-permute-done.2.one_ref
  28.9 4.3 %collective-permute-done.3.two_ref = f32[36,8,128]{2,1,0:T(8,128)S(1)} collective-permute-done((f32[36,8,128]{2,1,0:T(8,128)S(1)}, f32[36,8,128]{2,1,0:T(8,128)S(1)}, u32[]{:S(2)}, u32[]{:S(2)}) %collective-permute-start.3) | collective-permute-done | bytes 147488 | tf_op jit(solution)/shard_map/ppermute | solution.py:366
  33.2 0.0 copy-done.7
  33.2 0.0 copy-done.1
  33.2 0.0 copy-done.3
  33.2 0.0 copy-done.5
  33.2 5.7 %main.1 = (f32[16,8,128]{2,1,0:T(8,128)}, f32[16,8,128]{2,1,0:T(8,128)}, f32[32,128]{1,0:T(8,128)S(1)}) custom-call(f32[16,8,128]{2,1,0:T(8,128)S(1)} %copy-done.1, f32[16,8,128]{2,1,0:T(8,128)S(1)} %copy-done.3, f32[16,8,128]{2,1,0:T(8,128)S(1)} %copy-done.5, f32[16,8,128]{2,1,0:T(8,128)S(1)} %copy-done.7, f32[8,128]{1,0:T(8,128)S(1)} %copy-done.8, ...), custom_call_target="tpu_custom_call" | custom-call | flops 16777216 | bytes 1048576 | tf_op jit(solution)/shard_map/main/pallas_call | solution.py:399
  38.9 21.1 %all_to_all.5 = f32[32,1,128]{2,1,0:T(1,128)S(1)} all-to-all(f32[32,1,128]{2,1,0:T(1,128)S(1)} %bitcast.10), channel_id=1, replica_groups=mesh['gx'=32,'gy'=16] {'gx'}, dimensions={0} | all-to-all | bytes 32768 | tf_op jit(solution)/shard_map/all_to_all | solution.py:402
  60.0 0.9 %owner.1 = f32[2,1,256]{2,1,0:T(1,128)} custom-call(f32[32,128]{1,0:T(8,128)S(1)} %bitcast.9), custom_call_target="tpu_custom_call" | custom-call | flops 1048576 | bytes 1048576 | tf_op jit(solution)/shard_map/owner/pallas_call | solution.py:403
  (1 shorter events, 0.0 us)
Async XLA Ops:
  0.6 0.8 %copy-start = (f32[16,8,128]{2,1,0:T(8,128)S(1)}, f32[16,8,128]{2,1,0:T(8,128)}, u32[]{:S(2)}) copy-start(f32[16,8,128]{2,1,0:T(8,128)} %t_ref.3) | copy-start | bytes 196612
  1.5 0.8 %copy-start.2 = (f32[16,8,128]{2,1,0:T(8,128)S(1)}, f32[16,8,128]{2,1,0:T(8,128)}, u32[]{:S(2)}) copy-start(f32[16,8,128]{2,1,0:T(8,128)} %s_ref.3) | copy-start | bytes 196612
  2.3 0.8 %copy-start.4 = (f32[16,8,128]{2,1,0:T(8,128)S(1)}, f32[16,8,128]{2,1,0:T(8,128)}, u32[]{:S(2)}) copy-start(f32[16,8,128]{2,1,0:T(8,128)} %u_ref.3) | copy-start | bytes 196612
  3.2 0.8 %copy-start.6 = (f32[16,8,128]{2,1,0:T(8,128)S(1)}, f32[16,8,128]{2,1,0:T(8,128)}, u32[]{:S(2)}) copy-start(f32[16,8,128]{2,1,0:T(8,128)} %v_ref.3) | copy-start | bytes 196612
  4.0 0.7 %copy-start.8 = (f32[8,128]{1,0:T(8,128)S(1)}, f32[8,128]{1,0:T(8,128)}, u32[]{:S(2)}) copy-start(f32[8,128]{1,0:T(8,128)} %kap_ref.3) | copy-start | bytes 12292
  4.7 0.7 %copy-start.9 = (s32[8,128]{1,0:T(8,128)S(1)}, s32[8,128]{1,0:T(8,128)}, u32[]{:S(2)}) copy-start(s32[8,128]{1,0:T(8,128)} %dep_ref.5) | copy-start | bytes 12292
  5.5 13.4 %collective-permute-start = (f32[5,8,128]{2,1,0:T(8,128)S(1)}, f32[5,8,128]{2,1,0:T(8,128)S(1)}, u32[]{:S(2)}, u32[]{:S(2)}) collective-permute-start(f32[5,8,128]{2,1,0:T(8,128)S(1)} %get-tuple-element.18), channel_id=1, source_target_pairs={{0,16},{16,0},{32,48},{48,32},{64,80},{80,64},{96,112},{112,96},{1... | collective-permute-start | bytes 61448 | tf_op jit(solution)/shard_map/ppermute | solution.py:366
  7.4 13.0 %collective-permute-start.1 = (f32[5,8,128]{2,1,0:T(8,128)S(1)}, f32[5,8,128]{2,1,0:T(8,128)S(1)}, u32[]{:S(2)}, u32[]{:S(2)}) collective-permute-start(f32[5,8,128]{2,1,0:T(8,128)S(1)} %get-tuple-element.18), channel_id=1, source_target_pairs={{16,32},{32,16},{48,64},{64,48},{80,96},{96,80},{112,128},{128,112... | collective-permute-start | bytes 61448 | tf_op jit(solution)/shard_map/ppermute | solution.py:366
  20.4 7.8 %copy-start.10 = (f32[15,8,128]{2,1,0:T(8,128)S(1)}, f32[15,8,128]{2,1,0:T(8,128)}, u32[]{:S(2)}) copy-start(f32[15,8,128]{2,1,0:T(8,128)} %mix_ref.1) | copy-start | bytes 184324
  20.4 7.8 %copy-start.11 = (s32[1,8192]{1,0:T(1,128)S(1)}, s32[1,8192]{1,0:T(1,128)}, u32[]{:S(2)}) copy-start(s32[1,8192]{1,0:T(1,128)} %param.23) | copy-start | bytes 98308
  20.4 7.8 %copy-start.13 = (s32[1,2048]{1,0:T(1,128)S(1)}, s32[1,2048]{1,0:T(1,128)}, u32[]{:S(2)}) copy-start(s32[1,2048]{1,0:T(1,128)} %param.20) | copy-start | bytes 24580
  20.4 7.8 %copy-start.14 = (s32[1,2048]{1,0:T(1,128)S(1)}, s32[1,2048]{1,0:T(1,128)}, u32[]{:S(2)}) copy-start(s32[1,2048]{1,0:T(1,128)} %param.21) | copy-start | bytes 24580
  20.4 7.8 %copy-start.15 = (f32[64]{0:T(128)S(1)}, f32[64]{0:T(128)}, u32[]{:S(2)}) copy-start(f32[64]{0:T(128)} %param.22) | copy-start | bytes 772
  20.5 7.8 %copy-start.12 = (s32[1,2048]{1,0:T(1,128)S(1)}, s32[1,2048]{1,0:T(1,128)}, u32[]{:S(2)}) copy-start(s32[1,2048]{1,0:T(1,128)} %param.19) | copy-start | bytes 24580
  20.5 8.4 %collective-permute-start.2 = (f32[36,8,128]{2,1,0:T(8,128)S(1)}, f32[36,8,128]{2,1,0:T(8,128)S(1)}, u32[]{:S(2)}, u32[]{:S(2)}) collective-permute-start(f32[36,8,128]{2,1,0:T(8,128)S(1)} %get-tuple-element.21), channel_id=1, source_target_pairs={{0,1},{1,0},{2,3},{3,2},{4,5},{5,4},{6,7},{7,6},{8,9},{9,8},{10,11... | collective-permute-start | bytes 442376 | tf_op jit(solution)/shard_map/ppermute | solution.py:366
  24.0 9.1 %collective-permute-start.3 = (f32[36,8,128]{2,1,0:T(8,128)S(1)}, f32[36,8,128]{2,1,0:T(8,128)S(1)}, u32[]{:S(2)}, u32[]{:S(2)}) collective-permute-start(f32[36,8,128]{2,1,0:T(8,128)S(1)} %get-tuple-element.22), channel_id=1, source_target_pairs={{1,2},{2,1},{3,4},{4,3},{5,6},{6,5},{7,8},{8,7},{9,10},{10,9},{11,... | collective-permute-start | bytes 442376 | tf_op jit(solution)/shard_map/ppermute | solution.py:366
  28.2 5.0 %copy-start.7 = (f32[16,8,128]{2,1,0:T(8,128)S(1)}, f32[16,8,128]{2,1,0:T(8,128)}, u32[]{:S(2)}) copy-start(f32[16,8,128]{2,1,0:T(8,128)} %v_ref.3) | copy-start | bytes 196612
  28.3 4.9 %copy-start.1 = (f32[16,8,128]{2,1,0:T(8,128)S(1)}, f32[16,8,128]{2,1,0:T(8,128)}, u32[]{:S(2)}) copy-start(f32[16,8,128]{2,1,0:T(8,128)} %t_ref.3) | copy-start | bytes 196612
  28.3 4.9 %copy-start.3 = (f32[16,8,128]{2,1,0:T(8,128)S(1)}, f32[16,8,128]{2,1,0:T(8,128)}, u32[]{:S(2)}) copy-start(f32[16,8,128]{2,1,0:T(8,128)} %s_ref.3) | copy-start | bytes 196612
  28.3 4.9 %copy-start.5 = (f32[16,8,128]{2,1,0:T(8,128)S(1)}, f32[16,8,128]{2,1,0:T(8,128)}, u32[]{:S(2)}) copy-start(f32[16,8,128]{2,1,0:T(8,128)} %u_ref.3) | copy-start | bytes 196612

commit v2 on v1

--- a/solution.py
+++ b/solution.py
@@ -13,6 +13,13 @@
 BF16 = jnp.bfloat16
 
 
+LEAD = 20
+
+
+def seat(place):
+    return ((place >> 8) - LEAD) & 31
+
+
 def iota(shape, dim):
     return lax.broadcasted_iota(jnp.int32, shape, dim)
 
@@ -21,25 +28,22 @@
     return (((iota((ROWS, LANES), 0) >> 2) + parity) & 1) == 0
 
 
-def pack_kernel(t_ref, s_ref, u_ref, v_ref, kap_ref, dep_ref, col_ref, one_ref, two_ref):
+def pack_kernel(*refs):
+    sources, col_ref, held, sem = refs[:6], refs[6], refs[7:13], refs[13]
+    copies = [pltpu.make_async_copy(x, y, sem.at[i]) for i, (x, y) in enumerate(zip(sources, held))]
+    for copy in copies:
+        copy.start()
     slot = iota((ROWS, LANES), 1) >> 3
-    mask = row_mask(lax.axis_index("gy") & 1)
-    for a, ref in enumerate((t_ref, s_ref, u_ref, v_ref)):
+    for a in range(4):
+        copies[a].wait()
         strip = jnp.zeros((ROWS, LANES), F32)
         for k in range(LEVELS):
-            strip = jnp.where(slot == k, pltpu.roll(ref[k], (8 * k + 4) % LANES, 1), strip)
+            strip = jnp.where(slot == k, pltpu.roll(held[a][k], (8 * k + 4) % LANES, 1), strip)
         col_ref[a] = strip
-        for k in range(8):
-            here, there = ref[k], pltpu.roll(ref[k + 8], 4, 0)
-            one_ref[a * 8 + k] = jnp.where(mask, there, here)
-            two_ref[a * 8 + k] = jnp.where(mask, here, there)
-    kap = kap_ref[...]
-    dep = dep_ref[...].astype(F32)
-    strip = jnp.where(slot == 0, pltpu.roll(kap, 4, 1), jnp.zeros((ROWS, LANES), F32))
-    col_ref[4] = jnp.where(slot == 1, pltpu.roll(dep, 12, 1), strip)
-    there = pltpu.roll(dep, 4, 0)
-    one_ref[32] = jnp.where(mask, there, kap)
-    two_ref[32] = jnp.where(mask, kap, there)
+    copies[4].wait()
+    copies[5].wait()
+    strip = jnp.where(slot == 0, pltpu.roll(held[4][...], 4, 1), jnp.zeros((ROWS, LANES), F32))
+    col_ref[4] = jnp.where(slot == 1, pltpu.roll(held[5][...].astype(F32), 12, 1), strip)
 
 
 def side_columns(first_ref, second_ref):
@@ -48,17 +52,22 @@
     return [jnp.where(mask, second_ref[a], first_ref[a]) for a in range(5)]
 
 
-def corner_kernel(one_in, two_in, first_ref, second_ref, one_ref, two_ref):
-    for i in range(33):
-        one_ref[i] = one_in[i]
-        two_ref[i] = two_in[i]
+def rows_kernel(t_ref, s_ref, u_ref, v_ref, kap_ref, dep_ref, second_ref, first_ref, one_ref, two_ref):
+    mask = row_mask(lax.axis_index("gy") & 1)
+
+    def put(i, here, there):
+        there = pltpu.roll(there, 4, 0)
+        one_ref[i] = jnp.where(mask, there, here)
+        two_ref[i] = jnp.where(mask, here, there)
+
+    for a, ref in enumerate((t_ref, s_ref, u_ref, v_ref)):
+        for k in range(8):
+            put(a * 8 + k, ref[k], ref[k + 8])
+    put(32, kap_ref[...], dep_ref[...].astype(F32))
     side = side_columns(first_ref, second_ref)
     side.append(jnp.zeros((ROWS, LANES), F32))
-    mask = row_mask(lax.axis_index("gy") & 1)
     for i in range(3):
-        here, there = side[2 * i], pltpu.roll(side[2 * i + 1], 4, 0)
-        one_ref[33 + i] = jnp.where(mask, there, here)
-        two_ref[33 + i] = jnp.where(mask, here, there)
+        put(33 + i, side[2 * i], side[2 * i + 1])
 
 
 def prep_kernel(
@@ -124,11 +133,12 @@
         line = jnp.broadcast_to(place_ref[pl.ds(r * 16 + (q >> 1), 1), :], (ROWS, LANES))
         place = jnp.take_along_axis(line, (lane >> 1) + 64 * (q & 1), axis=1)
         own.append(place)
-        hot.append(jnp.where(jnp.broadcast_to(place[0:1] >> 8, (32, LANES)) == iota((32, LANES), 0), 1.0, 0.0))
+        hot.append(jnp.where(jnp.broadcast_to(seat(place[0:1]), (32, LANES)) == iota((32, LANES), 0), 1.0, 0.0))
         line = jnp.broadcast_to(place_ref[pl.ds(r * 16 + (nextq >> 1), 1), :], (ROWS, LANES))
         place = jnp.take_along_axis(line, (lane & 0) + 64 * (nextq & 1), axis=1)
         outside = jnp.where((lane >> 1) == r, place, outside)
-    hot.append(jnp.where(jnp.broadcast_to(outside[0:1] >> 8, (32, LANES)) == iota((32, LANES), 0), 1.0, 0.0))
+    line = jnp.where(outside[0:1] < 0, -1, seat(outside[0:1]))
+    hot.append(jnp.where(jnp.broadcast_to(line, (32, LANES)) == iota((32, LANES), 0), 1.0, 0.0))
     owner = jnp.concatenate(hot, axis=1).astype(BF16)
     owner_ref[...] = owner
     stacked = jnp.concatenate(hot[:4], axis=0).astype(BF16)
@@ -159,7 +169,7 @@
 
 
 def main_kernel(
-    t_ref, s_ref, u_ref, v_ref, kap_ref, dep_ref, first_ref, second_ref, one_ref, two_ref,
+    t_ref, s_ref, u_ref, v_ref, kap_ref, dep_ref, second_ref, first_ref, two_ref, one_ref,
     inv_ref, down_ref, up_ref, weight_ref, owner_ref, rank_ref, slot_ref,
     tout_ref, sout_ref, send_ref,
 ):
@@ -319,14 +329,14 @@
 
 
 def call(kernel, name, outs, n_in, flops, **kw):
+    kw.setdefault("in_specs", [VMEM] * n_in)
+    kw.setdefault("compiler_params", pltpu.CompilerParams(vmem_limit_bytes=16 << 20))
     return pl.pallas_call(
         kernel,
         name=name,
         out_shape=tuple(jax.ShapeDtypeStruct(s, d) for s, d in outs),
-        in_specs=[VMEM] * n_in,
         out_specs=tuple([VMEM] * len(outs)),
         cost_estimate=pl.CostEstimate(flops=flops, bytes_accessed=1 << 20, transcendentals=0),
-        compiler_params=pltpu.CompilerParams(vmem_limit_bytes=16 << 20),
         **kw,
     )
 
@@ -356,7 +366,16 @@
     )
     plane = (ROWS, LANES)
     strips = ((36,) + plane, F32)
-    column, one, two = call(pack_kernel, "pack", [((5,) + plane, F32), strips, strips], 6, 1 << 20)(*fields)
+    (column,) = call(
+        pack_kernel,
+        "pack",
+        [((5,) + plane, F32)],
+        6,
+        1 << 18,
+        in_specs=[pl.BlockSpec(memory_space=pltpu.HBM)] * 6,
+        scratch_shapes=[pltpu.VMEM(x.shape, x.dtype) for x in fields] + [pltpu.SemaphoreType.DMA((6,))],
+        compiler_params=None,
+    )(*fields)
 
     def swap(x, axis, count, start, wrap):
         pairs = []
@@ -365,13 +384,11 @@
                 pairs += [(i, (i + 1) % count), ((i + 1) % count, i)]
         return lax.ppermute(x, axis, pairs)
 
+    second = swap(column, "gx", nx, 1, True)
     first = swap(column, "gx", nx, 0, True)
-    second = swap(column, "gx", nx, 1, True)
-    one, two = call(corner_kernel, "corner", [strips, strips], 4, 1 << 16)(
-        one, two, first, second
-    )
+    one, two = call(rows_kernel, "rows", [strips, strips], 8, 1 << 16)(*fields, second, first)
+    two = swap(two, "gy", ny, 1, False)
     one = swap(one, "gy", ny, 0, False)
-    two = swap(two, "gy", ny, 1, False)
     column3 = ((LEVELS,) + plane, F32)
     prepared = call(
         prep_kernel,
@@ -398,8 +415,9 @@
     )
     temperature, salinity, send = call(
         main_kernel, "main", [column3, column3, ((32, LANES), F32)], 17, 1 << 24
-    )(*fields, first, second, one, two, *prepared)
-    got = lax.all_to_all(send.reshape(nx, 1, LANES), "gx", 0, 0, tiled=True)
+    )(*fields, second, first, two, one, *prepared)
+    order = [[(i + LEAD) % nx for i in range(nx)]]
+    got = lax.all_to_all(send.reshape(nx, 1, LANES), "gx", 0, 0, tiled=True, axis_index_groups=order)
     (air,) = call(owner_kernel, "owner", [((2, 1, 256), F32)], 1, 1 << 20)(got.reshape(nx, LANES))
     return temperature, salinity, air
 

time: 61.3 us -> 50.9 us (0.83)
  blocking collectives: 21.1 us -> 14.4 us
  local copies, waits for them, and re-layouts: 4.77 us -> 0.66 us
  Pallas kernels: 7.28 us -> 9.15 us
  starting transfers between devices: 21.1 us -> 19.7 us
    all_to_all x1, blocking collectives: 21.1 us -> 14.4 us  [shards(): lax.all_to_all(send.reshape(nx, 1, LANES), 'gx', 0, 0, tiled=True, axis_i...]
    unnamed x32 -> x24, local copies, waits for them, and re-layouts: 4.77 us -> 0.66 us
    pallas_call x2, Pallas kernels: 0.16 us -> 2.04 us  [the longest x1 2.01 us: shards(): call(pack_kernel, 'pack', [((5,) + plane, F32)], 6, 1 << 18, in_specs=[pl...]
    ppermute x4, starting transfers between devices: 21.1 us -> 19.7 us  [swap(): return lax.ppermute(x, axis, pairs)]
  transfers between devices with their start and end apart: 4 -> 4, of which waited for: 2 -> 3; matrix products, arithmetic and copies ran while one was open for 0% -> 0% of each run, Pallas kernels for 1% -> 1%
where the time goes in v2:
time: 50.9 us; the launch traced here: 50.5 us
  starting transfers between devices  19.7 us (39%)
  blocking collectives  14.4 us (28%)
  Pallas kernels  9.15 us (18%)
  waiting for transfers between devices  5.72 us (11%)
  between operations  0.85 us (2%)
  local copies, waits for them, and re-layouts  0.66 us (1%)
    ppermute x4, starting transfers between devices, swap(): return lax.ppermute(x, axis, pairs)  19.7 us
    all_to_all x1, blocking collectives, shards(): lax.all_to_all(send.reshape(nx, 1, LANES), 'gx', 0, 0, tiled=True, axis_i...  14.4 us
    ppermute x4, waiting for transfers between devices, swap(): return lax.ppermute(x, axis, pairs)  5.72 us
    pallas_call x1, Pallas kernels, shards(): call(main_kernel, 'main', [column3, column3, ((32, LANES), F32)], 17, 1 <...  5.71 us
    pallas_call x1, Pallas kernels, shards(): call(pack_kernel, 'pack', [((5,) + plane, F32)], 6, 1 << 18, in_specs=[pl...  2.01 us
  transfers between devices with their start and end apart: 4, of which 3 were waited for; matrix products, arithmetic and copies ran while one was open for 0% of the time, Pallas kernels for 1%

profile of v2, /device:TPU:24, one launch (start us, length us, event | category | flops | bytes accessed | tf_op | source)
XLA Modules:
  0.0 50.5 jit_solution(1305495253770256254)
XLA Ops:
  0.6 0.0 copy-start
  0.6 0.0 copy-start.1
  0.7 0.0 copy-start.2
  0.7 0.0 copy-start.3
  0.7 0.0 copy-start.4
  0.7 0.0 copy-start.5
  0.7 2.0 %pack.1 = f32[5,8,128]{2,1,0:T(8,128)} custom-call(f32[16,8,128]{2,1,0:T(8,128)} %t_ref.3, f32[16,8,128]{2,1,0:T(8,128)} %s_ref.3, f32[16,8,128]{2,1,0:T(8,128)} %u_ref.3, f32[16,8,128]{2,1,0:T(8,128)} %v_ref.3, f32[8,128]{1,0:T(8,128)} %kap_ref.3, s32[8,128]{1,0:T(8,128)} %dep_ref.5), custom_call_target="tpu_custom_call" | custom-call | flops 262144 | bytes 1048576 | tf_op jit(solution)/shard_map/pack/pallas_call | solution.py:369
  2.7 0.0 copy-start.6
  2.7 0.0 copy-start.7
  2.7 11.0 %collective-permute-start = (f32[5,8,128]{2,1,0:T(8,128)}, f32[5,8,128]{2,1,0:T(8,128)S(1)}, u32[]{:S(2)}, u32[]{:S(2)}) collective-permute-start(f32[5,8,128]{2,1,0:T(8,128)} %pack.1), channel_id=1, source_target_pairs={{16,32},{32,16},{48,64},{64,48},{80,96},{96,80},{112,128},{128,112... | collective-permute-start | bytes 61448 | tf_op jit(solution)/shard_map/ppermute | solution.py:385
  13.7 1.9 %collective-permute-start.1 = (f32[5,8,128]{2,1,0:T(8,128)}, f32[5,8,128]{2,1,0:T(8,128)S(1)}, u32[]{:S(2)}, u32[]{:S(2)}) collective-permute-start(f32[5,8,128]{2,1,0:T(8,128)} %pack.1), channel_id=1, source_target_pairs={{0,16},{16,0},{32,48},{48,32},{64,80},{80,64},{96,112},{112,96},{1... | collective-permute-start | bytes 61448 | tf_op jit(solution)/shard_map/ppermute | solution.py:385
  15.6 0.0 collective-permute-done.second_ref
  15.7 1.4 %collective-permute-done.1.first_ref = f32[5,8,128]{2,1,0:T(8,128)S(1)} collective-permute-done((f32[5,8,128]{2,1,0:T(8,128)}, f32[5,8,128]{2,1,0:T(8,128)S(1)}, u32[]{:S(2)}, u32[]{:S(2)}) %collective-permute-start.1) | collective-permute-done | bytes 20512 | tf_op jit(solution)/shard_map/ppermute | solution.py:385
  17.0 0.0 copy-done
  17.0 0.0 copy-done.1
  17.0 0.0 copy-done.2
  17.0 0.0 copy-done.3
  17.0 0.0 copy-done.4
  17.0 0.0 copy-done.5
  17.0 0.0 copy-start.9
  17.1 0.0 copy-start.10
  17.1 0.0 copy-start.8
  17.1 4.8 %collective-permute-start.2 = (f32[36,8,128]{2,1,0:T(8,128)S(1)}, f32[36,8,128]{2,1,0:T(8,128)S(1)}, u32[]{:S(2)}, u32[]{:S(2)}) collective-permute-start(f32[36,8,128]{2,1,0:T(8,128)S(1)} %get-tuple-element.15), channel_id=1, source_target_pairs={{1,2},{2,1},{3,4},{4,3},{5,6},{6,5},{7,8},{8,7},{9,10},{10,9},{11,... | collective-permute-start | bytes 442376 | tf_op jit(solution)/shard_map/ppermute | solution.py:385
  22.0 2.0 %collective-permute-start.3 = (f32[36,8,128]{2,1,0:T(8,128)S(1)}, f32[36,8,128]{2,1,0:T(8,128)S(1)}, u32[]{:S(2)}, u32[]{:S(2)}) collective-permute-start(f32[36,8,128]{2,1,0:T(8,128)S(1)} %get-tuple-element.16), channel_id=1, source_target_pairs={{0,1},{1,0},{2,3},{3,2},{4,5},{5,4},{6,7},{7,6},{8,9},{9,8},{10,11... | collective-permute-start | bytes 442376 | tf_op jit(solution)/shard_map/ppermute | solution.py:385
  23.9 0.0 copy-start.11
  24.0 0.0 copy-done.6
  24.0 0.0 copy-done.7
  24.0 0.0 copy-done.9
  24.0 0.0 copy-done.10
  24.0 0.0 copy-done.8
  24.0 0.6 %copy-done.11 = f32[64]{0:T(128)S(1)} copy-done((f32[64]{0:T(128)S(1)}, f32[64]{0:T(128)}, u32[]{:S(2)}) %copy-start.11) | copy-done | bytes 280
  24.6 0.5 %prep.1 = (f32[16,8,128]{2,1,0:T(8,128)S(1)}, f32[16,8,128]{2,1,0:T(8,128)S(1)}, f32[16,8,128]{2,1,0:T(8,128)S(1)}, f32[4,8,128]{2,1,0:T(8,128)S(1)}, bf16[32,64...) custom-call(s32[16,128]{1,0:T(8,128)S(1)} %bitcast.12, s32[16,128]{1,0:T(8,128)S(1)} %bitcast.13, ...), custom_call_target="tpu_custom_call" | custom-call | flops 67108864 | bytes 1048576 | tf_op jit(solution)/shard_map/prep/pallas_call | solution.py:393
  25.1 1.9 %collective-permute-done.2.two_ref = f32[36,8,128]{2,1,0:T(8,128)S(1)} collective-permute-done((f32[36,8,128]{2,1,0:T(8,128)S(1)}, f32[36,8,128]{2,1,0:T(8,128)S(1)}, u32[]{:S(2)}, u32[]{:S(2)}) %collective-permute-start.2) | collective-permute-done | bytes 147488 | tf_op jit(solution)/shard_map/ppermute | solution.py:385
  27.0 2.5 %collective-permute-done.3.one_ref = f32[36,8,128]{2,1,0:T(8,128)S(1)} collective-permute-done((f32[36,8,128]{2,1,0:T(8,128)S(1)}, f32[36,8,128]{2,1,0:T(8,128)S(1)}, u32[]{:S(2)}, u32[]{:S(2)}) %collective-permute-start.3) | collective-permute-done | bytes 147488 | tf_op jit(solution)/shard_map/ppermute | solution.py:385
  29.5 5.7 %main.1 = (f32[16,8,128]{2,1,0:T(8,128)}, f32[16,8,128]{2,1,0:T(8,128)}, f32[32,128]{1,0:T(8,128)S(1)}) custom-call(f32[16,8,128]{2,1,0:T(8,128)S(1)} %copy-done, f32[16,8,128]{2,1,0:T(8,128)S(1)} %copy-done.1, f32[16,8,128]{2,1,0:T(8,128)S(1)} %copy-done.2, f32[16,8,128]{2,1,0:T(8,128)S(1)} %copy-done.3, f32[8,128]{1,0:T(8,128)S(1)} %copy-done.4, ...), custom_call_target="tpu_custom_call" | custom-call | flops 16777216 | bytes 1048576 | tf_op jit(solution)/shard_map/main/pallas_call | solution.py:416
  35.2 14.4 %all_to_all.5 = f32[32,1,128]{2,1,0:T(1,128)S(1)} all-to-all(f32[32,1,128]{2,1,0:T(1,128)S(1)} %bitcast.10), channel_id=1, replica_groups={{320,336,352,368,384,400,416,432,448,464,480,496,0,16,32,48,64,80,96,11..., dimensions={0} | all-to-all | bytes 32768 | tf_op jit(solution)/shard_map/all_to_all | solution.py:420
  49.6 0.9 %owner.1 = f32[2,1,256]{2,1,0:T(1,128)} custom-call(f32[32,128]{1,0:T(8,128)S(1)} %bitcast.9), custom_call_target="tpu_custom_call" | custom-call | flops 1048576 | bytes 1048576 | tf_op jit(solution)/shard_map/owner/pallas_call | solution.py:421
  (1 shorter events, 0.0 us)
Async XLA Ops:
  0.6 16.4 %copy-start = (f32[16,8,128]{2,1,0:T(8,128)S(1)}, f32[16,8,128]{2,1,0:T(8,128)}, u32[]{:S(2)}) copy-start(f32[16,8,128]{2,1,0:T(8,128)} %t_ref.3) | copy-start | bytes 196612
  0.6 16.4 %copy-start.1 = (f32[16,8,128]{2,1,0:T(8,128)S(1)}, f32[16,8,128]{2,1,0:T(8,128)}, u32[]{:S(2)}) copy-start(f32[16,8,128]{2,1,0:T(8,128)} %s_ref.3) | copy-start | bytes 196612
  0.7 16.4 %copy-start.2 = (f32[16,8,128]{2,1,0:T(8,128)S(1)}, f32[16,8,128]{2,1,0:T(8,128)}, u32[]{:S(2)}) copy-start(f32[16,8,128]{2,1,0:T(8,128)} %u_ref.3) | copy-start | bytes 196612
  0.7 16.4 %copy-start.3 = (f32[16,8,128]{2,1,0:T(8,128)S(1)}, f32[16,8,128]{2,1,0:T(8,128)}, u32[]{:S(2)}) copy-start(f32[16,8,128]{2,1,0:T(8,128)} %v_ref.3) | copy-start | bytes 196612
  0.7 16.4 %copy-start.4 = (f32[8,128]{1,0:T(8,128)S(1)}, f32[8,128]{1,0:T(8,128)}, u32[]{:S(2)}) copy-start(f32[8,128]{1,0:T(8,128)} %kap_ref.3) | copy-start | bytes 12292
  0.7 16.4 %copy-start.5 = (s32[8,128]{1,0:T(8,128)S(1)}, s32[8,128]{1,0:T(8,128)}, u32[]{:S(2)}) copy-start(s32[8,128]{1,0:T(8,128)} %dep_ref.5) | copy-start | bytes 12292
  2.7 21.2 %copy-start.6 = (f32[15,8,128]{2,1,0:T(8,128)S(1)}, f32[15,8,128]{2,1,0:T(8,128)}, u32[]{:S(2)}) copy-start(f32[15,8,128]{2,1,0:T(8,128)} %mix_ref.1) | copy-start | bytes 184324
  2.7 21.2 %copy-start.7 = (s32[1,8192]{1,0:T(1,128)S(1)}, s32[1,8192]{1,0:T(1,128)}, u32[]{:S(2)}) copy-start(s32[1,8192]{1,0:T(1,128)} %param.23) | copy-start | bytes 98308
  2.7 12.9 %collective-permute-start = (f32[5,8,128]{2,1,0:T(8,128)}, f32[5,8,128]{2,1,0:T(8,128)S(1)}, u32[]{:S(2)}, u32[]{:S(2)}) collective-permute-start(f32[5,8,128]{2,1,0:T(8,128)} %pack.1), channel_id=1, source_target_pairs={{16,32},{32,16},{48,64},{64,48},{80,96},{96,80},{112,128},{128,112... | collective-permute-start | bytes 61448 | tf_op jit(solution)/shard_map/ppermute | solution.py:385
  13.7 3.3 %collective-permute-start.1 = (f32[5,8,128]{2,1,0:T(8,128)}, f32[5,8,128]{2,1,0:T(8,128)S(1)}, u32[]{:S(2)}, u32[]{:S(2)}) collective-permute-start(f32[5,8,128]{2,1,0:T(8,128)} %pack.1), channel_id=1, source_target_pairs={{0,16},{16,0},{32,48},{48,32},{64,80},{80,64},{96,112},{112,96},{1... | collective-permute-start | bytes 61448 | tf_op jit(solution)/shard_map/ppermute | solution.py:385
  17.0 6.9 %copy-start.9 = (s32[1,2048]{1,0:T(1,128)S(1)}, s32[1,2048]{1,0:T(1,128)}, u32[]{:S(2)}) copy-start(s32[1,2048]{1,0:T(1,128)} %param.20) | copy-start | bytes 24580
  17.1 6.9 %copy-start.10 = (s32[1,2048]{1,0:T(1,128)S(1)}, s32[1,2048]{1,0:T(1,128)}, u32[]{:S(2)}) copy-start(s32[1,2048]{1,0:T(1,128)} %param.21) | copy-start | bytes 24580
  17.1 6.9 %copy-start.8 = (s32[1,2048]{1,0:T(1,128)S(1)}, s32[1,2048]{1,0:T(1,128)}, u32[]{:S(2)}) copy-start(s32[1,2048]{1,0:T(1,128)} %param.19) | copy-start | bytes 24580
  17.1 9.9 %collective-permute-start.2 = (f32[36,8,128]{2,1,0:T(8,128)S(1)}, f32[36,8,128]{2,1,0:T(8,128)S(1)}, u32[]{:S(2)}, u32[]{:S(2)}) collective-permute-start(f32[36,8,128]{2,1,0:T(8,128)S(1)} %get-tuple-element.15), channel_id=1, source_target_pairs={{1,2},{2,1},{3,4},{4,3},{5,6},{6,5},{7,8},{8,7},{9,10},{10,9},{11,... | collective-permute-start | bytes 442376 | tf_op jit(solution)/shard_map/ppermute | solution.py:385
  22.0 7.5 %collective-permute-start.3 = (f32[36,8,128]{2,1,0:T(8,128)S(1)}, f32[36,8,128]{2,1,0:T(8,128)S(1)}, u32[]{:S(2)}, u32[]{:S(2)}) collective-permute-start(f32[36,8,128]{2,1,0:T(8,128)S(1)} %get-tuple-element.16), channel_id=1, source_target_pairs={{0,1},{1,0},{2,3},{3,2},{4,5},{5,4},{6,7},{7,6},{8,9},{9,8},{10,11... | collective-permute-start | bytes 442376 | tf_op jit(solution)/shard_map/ppermute | solution.py:385
  23.9 0.7 %copy-start.11 = (f32[64]{0:T(128)S(1)}, f32[64]{0:T(128)}, u32[]{:S(2)}) copy-start(f32[64]{0:T(128)} %param.22) | copy-start | bytes 772

commit v3 on v2

--- a/solution.py
+++ b/solution.py
@@ -171,7 +171,7 @@
 def main_kernel(
     t_ref, s_ref, u_ref, v_ref, kap_ref, dep_ref, second_ref, first_ref, two_ref, one_ref,
     inv_ref, down_ref, up_ref, weight_ref, owner_ref, rank_ref, slot_ref,
-    tout_ref, sout_ref, send_ref,
+    tout_ref, sout_ref, send_ref, strip_ref, face_ref,
 ):
     shape = (ROWS, LANES)
     lane, sub = iota(shape, 1), iota(shape, 0)
@@ -212,57 +212,69 @@
     for i in range(3):
         corner.extend(pair(33 + i))
 
+    for i in range(5):
+        strip_ref[0, i] = side[i]
+        strip_ref[1, i] = corner[i]
+
     def field(local, plane, k, outer):
-        shift = (LANES - 8 * k - 4) % LANES
-        return local, pltpu.roll(side[plane], shift, 1), outer, pltpu.roll(corner[plane], shift, 1)
+        shift = (2 * LANES - 8 * k - 4) % LANES if isinstance(k, int) else (2 * LANES - 4) - 8 * k
+        strips = [pltpu.roll(strip_ref[i, plane], shift, 1) for i in range(2)]
+        return local, strips[0], outer, strips[1]
 
     outer_kap, outer_dep = pair(32)
     kap = field(kap_ref[...], 4, 0, outer_kap)
     dep = field(dep_ref[...].astype(F32), 4, 1, outer_dep)
-    kap_east = [0.5 * (x + y) for x, y in zip(kap, east(kap))]
-    kap_north = [0.5 * (x + y) for x, y in zip(kap, north(kap))]
-    dep_east = [jnp.minimum(x, y) for x, y in zip(dep, east(dep))]
-    dep_north = [jnp.minimum(x, y) for x, y in zip(dep, north(dep))]
+    faces = (
+        [0.5 * (x + y) for x, y in zip(kap, east(kap))],
+        [0.5 * (x + y) for x, y in zip(kap, north(kap))],
+        [jnp.minimum(x, y) for x, y in zip(dep, east(dep))],
+        [jnp.minimum(x, y) for x, y in zip(dep, north(dep))],
+    )
+    for i, face in enumerate(faces):
+        for j in range(4):
+            face_ref[i, j] = face[j]
 
     def level(k, outer):
         u = field(u_ref[k], 2, k, outer[2])
         v = field(v_ref[k], 3, k, outer[3])
-        level_f = float(k)
-
-        def face(rate, kappa, depth):
-            here = [
-                jnp.where(d > level_f, jnp.maximum(r, 0.0) + c, 0.0) for r, c, d in zip(rate, kappa, depth)
-            ]
-            there = [
-                jnp.where(d > level_f, c - jnp.minimum(r, 0.0), 0.0) for r, c, d in zip(rate, kappa, depth)
-            ]
+        level_f = lax.convert_element_type(k, F32)
+
+        def face(rate, which):
+            here, there = [], []
+            for i, r in enumerate(rate):
+                c = face_ref[which, i]
+                wet = face_ref[which + 2, i] > level_f
+                here.append(jnp.where(wet, jnp.maximum(r, 0.0) + c, 0.0))
+                there.append(jnp.where(wet, c - jnp.minimum(r, 0.0), 0.0))
             return here, there
 
-        here_e, from_e = face(u, kap_east, dep_east)
-        here_n, from_n = face(v, kap_north, dep_north)
+        here_e, from_e = face(u, 0)
+        here_n, from_n = face(v, 1)
         from_w = west(here_e)
         from_s = south(here_n)
         back_e = west(from_e)
         back_n = south(from_n)
-        keep = [
-            1.0 - ((a + b) + (c + d)) for a, b, c, d in zip(here_e, back_e, here_n, back_n)
-        ]
-        for which, (in_ref, out_ref) in enumerate(((t_ref, tout_ref), (s_ref, sout_ref))):
-            c = field(in_ref[k], which, k, outer[which])
-            for step in range(NSUB):
+        keep = [1.0 - ((a + b) + (c + d)) for a, b, c, d in zip(here_e, back_e, here_n, back_n)]
+        cells = [field(ref[k], i, k, outer[i]) for i, ref in enumerate((t_ref, s_ref))]
+        for step in range(NSUB):
+            for i, c in enumerate(cells):
                 around = zip(keep, c, from_e, east(c), from_w, west(c), from_n, north(c), from_s, south(c))
                 new = []
                 for c0, x, ce, xe, cw, xw, cn, xn, cs, xs in around:
                     new.append((c0 * x + (ce * xe + cw * xw)) + (cn * xn + cs * xs))
                     if step == NSUB - 1:
                         break
-                c = new
-            out_ref[k] = c[0]
-
-    for k in range(8):
+                cells[i] = new
+        tout_ref[k] = cells[0][0]
+        sout_ref[k] = cells[1][0]
+
+    def two_levels(k, nothing):
         pairs = [pair(a * 8 + k) for a in range(4)]
         level(k, [p[0] for p in pairs])
         level(k + 8, [p[1] for p in pairs])
+        return nothing
+
+    lax.fori_loop(0, 8, two_levels, 0, unroll=2)
 
     tops = []
     for out_ref in (tout_ref, sout_ref):
@@ -366,16 +378,15 @@
     )
     plane = (ROWS, LANES)
     strips = ((36,) + plane, F32)
-    (column,) = call(
+    column, *held = call(
         pack_kernel,
         "pack",
-        [((5,) + plane, F32)],
+        [((5,) + plane, F32)] + [(x.shape, x.dtype) for x in fields],
         6,
         1 << 18,
         in_specs=[pl.BlockSpec(memory_space=pltpu.HBM)] * 6,
-        scratch_shapes=[pltpu.VMEM(x.shape, x.dtype) for x in fields] + [pltpu.SemaphoreType.DMA((6,))],
-        compiler_params=None,
-    )(*fields)
+        scratch_shapes=[pltpu.SemaphoreType.DMA((6,))],
+    )(*[pltpu.with_memory_space_constraint(x, pltpu.HBM) for x in fields])
 
     def swap(x, axis, count, start, wrap):
         pairs = []
@@ -386,7 +397,7 @@
 
     second = swap(column, "gx", nx, 1, True)
     first = swap(column, "gx", nx, 0, True)
-    one, two = call(rows_kernel, "rows", [strips, strips], 8, 1 << 16)(*fields, second, first)
+    one, two = call(rows_kernel, "rows", [strips, strips], 8, 1 << 16)(*held, second, first)
     two = swap(two, "gy", ny, 1, False)
     one = swap(one, "gy", ny, 0, False)
     column3 = ((LEVELS,) + plane, F32)
@@ -411,11 +422,16 @@
         patch_measures.reshape(1, 64),
         holder_ordering.reshape(64, LANES),
         stratum_interface_mixing,
-        flooded_strata,
+        held[5],
     )
     temperature, salinity, send = call(
-        main_kernel, "main", [column3, column3, ((32, LANES), F32)], 17, 1 << 24
-    )(*fields, second, first, two, one, *prepared)
+        main_kernel,
+        "main",
+        [column3, column3, ((32, LANES), F32)],
+        17,
+        1 << 24,
+        scratch_shapes=[pltpu.VMEM((2, 5) + plane, F32), pltpu.VMEM((4, 4) + plane, F32)],
+    )(*held, second, first, two, one, *prepared)
     order = [[(i + LEAD) % nx for i in range(nx)]]
     got = lax.all_to_all(send.reshape(nx, 1, LANES), "gx", 0, 0, tiled=True, axis_index_groups=order)
     (air,) = call(owner_kernel, "owner", [((2, 1, 256), F32)], 1, 1 << 20)(got.reshape(nx, LANES))

time: 50.9 us -> 47.3 us (0.929)
  Pallas kernels: 9.15 us -> 5.97 us
    pallas_call x1, Pallas kernels: 5.71 us -> 3.23 us  [shards(): call(main_kernel, 'main', [column3, column3, ((32, LANES), F32)], 17, 1 <...]
    pallas_call x1, Pallas kernels: 2.01 us -> 1.31 us  [shards(): call(pack_kernel, 'pack', [((5,) + plane, F32)] + [(x.shape, x.dtype) for...]
where the time goes in v3:
time: 47.3 us; the launch traced here: 47 us
  starting transfers between devices  19.7 us (42%)
  blocking collectives  14.4 us (30%)
  Pallas kernels  5.97 us (13%)
  waiting for transfers between devices  5.51 us (12%)
  between operations  0.75 us (2%)
  local copies, waits for them, and re-layouts  0.62 us (1%)
    ppermute x4, starting transfers between devices, swap(): return lax.ppermute(x, axis, pairs)  19.7 us
    all_to_all x1, blocking collectives, shards(): lax.all_to_all(send.reshape(nx, 1, LANES), 'gx', 0, 0, tiled=True, axis_i...  14.4 us
    ppermute x4, waiting for transfers between devices, swap(): return lax.ppermute(x, axis, pairs)  5.51 us
    pallas_call x1, Pallas kernels, shards(): call(main_kernel, 'main', [column3, column3, ((32, LANES), F32)], 17, 1 <...  3.23 us
    pallas_call x1, Pallas kernels, shards(): call(pack_kernel, 'pack', [((5,) + plane, F32)] + [(x.shape, x.dtype) for...  1.31 us
  transfers between devices with their start and end apart: 4, of which 3 were waited for; matrix products, arithmetic and copies ran while one was open for 0% of the time, Pallas kernels for 1%

profile of v3, /device:TPU:24, one launch (start us, length us, event | category | flops | bytes accessed | tf_op | source)
XLA Modules:
  0.0 47.0 jit_solution(9959438253991625096)
XLA Ops:
  0.6 1.3 %pack.1 = (f32[5,8,128]{2,1,0:T(8,128)S(1)}, f32[16,8,128]{2,1,0:T(8,128)S(1)}, f32[16,8,128]{2,1,0:T(8,128)S(1)}, f32[16,8,128]{2,1,0:T(8,128)S(1)}, f32[16,8,1...) custom-call(f32[16,8,128]{2,1,0:T(8,128)} %refs_0_.1, f32[16,8,128]{2,1,0:T(8,128)} %refs_1_.1, ...), custom_call_target="tpu_custom_call" | custom-call | flops 262144 | bytes 1048576 | tf_op jit(solution)/shard_map/pack/pallas_call | solution.py:381
  1.9 10.8 %collective-permute-start = (f32[5,8,128]{2,1,0:T(8,128)S(1)}, f32[5,8,128]{2,1,0:T(8,128)S(1)}, u32[]{:S(2)}, u32[]{:S(2)}) collective-permute-start(f32[5,8,128]{2,1,0:T(8,128)S(1)} %get-tuple-element.28), channel_id=1, source_target_pairs={{16,32},{32,16},{48,64},{64,48},{80,96},{96,80},{112,128},{128,112... | collective-permute-start | bytes 61448 | tf_op jit(solution)/shard_map/ppermute | solution.py:396
  12.8 1.9 %collective-permute-start.1 = (f32[5,8,128]{2,1,0:T(8,128)S(1)}, f32[5,8,128]{2,1,0:T(8,128)S(1)}, u32[]{:S(2)}, u32[]{:S(2)}) collective-permute-start(f32[5,8,128]{2,1,0:T(8,128)S(1)} %get-tuple-element.28), channel_id=1, source_target_pairs={{0,16},{16,0},{32,48},{48,32},{64,80},{80,64},{96,112},{112,96},{1... | collective-permute-start | bytes 61448 | tf_op jit(solution)/shard_map/ppermute | solution.py:396
  14.7 0.0 collective-permute-done.second_ref
  14.7 1.1 %collective-permute-done.1.first_ref = f32[5,8,128]{2,1,0:T(8,128)S(1)} collective-permute-done((f32[5,8,128]{2,1,0:T(8,128)S(1)}, f32[5,8,128]{2,1,0:T(8,128)S(1)}, u32[]{:S(2)}, u32[]{:S(2)}) %collective-permute-start.1) | collective-permute-done | bytes 20512 | tf_op jit(solution)/shard_map/ppermute | solution.py:396
  15.9 0.0 copy-start
  15.9 0.0 copy-start.1
  15.9 0.0 copy-start.3
  15.9 0.0 copy-start.4
  15.9 0.0 copy-start.2
  15.9 5.0 %collective-permute-start.2 = (f32[36,8,128]{2,1,0:T(8,128)S(1)}, f32[36,8,128]{2,1,0:T(8,128)S(1)}, u32[]{:S(2)}, u32[]{:S(2)}) collective-permute-start(f32[36,8,128]{2,1,0:T(8,128)S(1)} %get-tuple-element.29), channel_id=1, source_target_pairs={{1,2},{2,1},{3,4},{4,3},{5,6},{6,5},{7,8},{8,7},{9,10},{10,9},{11,... | collective-permute-start | bytes 442376 | tf_op jit(solution)/shard_map/ppermute | solution.py:396
  20.9 2.0 %collective-permute-start.3 = (f32[36,8,128]{2,1,0:T(8,128)S(1)}, f32[36,8,128]{2,1,0:T(8,128)S(1)}, u32[]{:S(2)}, u32[]{:S(2)}) collective-permute-start(f32[36,8,128]{2,1,0:T(8,128)S(1)} %get-tuple-element.30), channel_id=1, source_target_pairs={{0,1},{1,0},{2,3},{3,2},{4,5},{5,4},{6,7},{7,6},{8,9},{9,8},{10,11... | collective-permute-start | bytes 442376 | tf_op jit(solution)/shard_map/ppermute | solution.py:396
  22.9 0.0 copy-start.5
  22.9 0.0 copy-done
  22.9 0.0 copy-done.1
  22.9 0.0 copy-done.3
  22.9 0.0 copy-done.4
  22.9 0.0 copy-done.2
  23.0 0.6 %copy-done.5 = f32[64]{0:T(128)S(1)} copy-done((f32[64]{0:T(128)S(1)}, f32[64]{0:T(128)}, u32[]{:S(2)}) %copy-start.5) | copy-done | bytes 280
  23.6 0.5 %prep.1 = (f32[16,8,128]{2,1,0:T(8,128)S(1)}, f32[16,8,128]{2,1,0:T(8,128)S(1)}, f32[16,8,128]{2,1,0:T(8,128)S(1)}, f32[4,8,128]{2,1,0:T(8,128)S(1)}, bf16[32,64...) custom-call(s32[16,128]{1,0:T(8,128)S(1)} %bitcast.12, s32[16,128]{1,0:T(8,128)S(1)} %bitcast.13, ...), custom_call_target="tpu_custom_call" | custom-call | flops 67108864 | bytes 1048576 | tf_op jit(solution)/shard_map/prep/pallas_call | solution.py:404
  24.1 1.9 %collective-permute-done.2.two_ref = f32[36,8,128]{2,1,0:T(8,128)S(1)} collective-permute-done((f32[36,8,128]{2,1,0:T(8,128)S(1)}, f32[36,8,128]{2,1,0:T(8,128)S(1)}, u32[]{:S(2)}, u32[]{:S(2)}) %collective-permute-start.2) | collective-permute-done | bytes 147488 | tf_op jit(solution)/shard_map/ppermute | solution.py:396
  26.0 2.5 %collective-permute-done.3.one_ref = f32[36,8,128]{2,1,0:T(8,128)S(1)} collective-permute-done((f32[36,8,128]{2,1,0:T(8,128)S(1)}, f32[36,8,128]{2,1,0:T(8,128)S(1)}, u32[]{:S(2)}, u32[]{:S(2)}) %collective-permute-start.3) | collective-permute-done | bytes 147488 | tf_op jit(solution)/shard_map/ppermute | solution.py:396
  28.5 3.2 %main.1 = (f32[16,8,128]{2,1,0:T(8,128)}, f32[16,8,128]{2,1,0:T(8,128)}, f32[32,128]{1,0:T(8,128)S(1)}) custom-call(f32[16,8,128]{2,1,0:T(8,128)S(1)} %get-tuple-element.22.t_ref, f32[16,8,128]{2,1,0:T(8,128)S(1)} %get-tuple-element.23.s_ref, f32[16,8,128]{2,1,0:T(8,128)S(1)} %get-tuple-element.24.u_ref, f32[16,8,128]{2,1,0:T(8,128)S(1)} %get-tuple-element.25.v_ref, ...), custom_call_target="tpu_custom_call" | custom-call | flops 16777216 | bytes 1048576 | tf_op jit(solution)/shard_map/main/pallas_call | solution.py:427
  31.7 14.4 %all_to_all.5 = f32[32,1,128]{2,1,0:T(1,128)S(1)} all-to-all(f32[32,1,128]{2,1,0:T(1,128)S(1)} %bitcast.10), channel_id=1, replica_groups={{320,336,352,368,384,400,416,432,448,464,480,496,0,16,32,48,64,80,96,11..., dimensions={0} | all-to-all | bytes 32768 | tf_op jit(solution)/shard_map/all_to_all | solution.py:436
  46.1 0.9 %owner.1 = f32[2,1,256]{2,1,0:T(1,128)} custom-call(f32[32,128]{1,0:T(8,128)S(1)} %bitcast.9), custom_call_target="tpu_custom_call" | custom-call | flops 1048576 | bytes 1048576 | tf_op jit(solution)/shard_map/owner/pallas_call | solution.py:437
  (1 shorter events, 0.0 us)
Async XLA Ops:
  1.9 12.8 %collective-permute-start = (f32[5,8,128]{2,1,0:T(8,128)S(1)}, f32[5,8,128]{2,1,0:T(8,128)S(1)}, u32[]{:S(2)}, u32[]{:S(2)}) collective-permute-start(f32[5,8,128]{2,1,0:T(8,128)S(1)} %get-tuple-element.28), channel_id=1, source_target_pairs={{16,32},{32,16},{48,64},{64,48},{80,96},{96,80},{112,128},{128,112... | collective-permute-start | bytes 61448 | tf_op jit(solution)/shard_map/ppermute | solution.py:396
  12.8 3.1 %collective-permute-start.1 = (f32[5,8,128]{2,1,0:T(8,128)S(1)}, f32[5,8,128]{2,1,0:T(8,128)S(1)}, u32[]{:S(2)}, u32[]{:S(2)}) collective-permute-start(f32[5,8,128]{2,1,0:T(8,128)S(1)} %get-tuple-element.28), channel_id=1, source_target_pairs={{0,16},{16,0},{32,48},{48,32},{64,80},{80,64},{96,112},{112,96},{1... | collective-permute-start | bytes 61448 | tf_op jit(solution)/shard_map/ppermute | solution.py:396
  15.9 7.0 %copy-start = (f32[15,8,128]{2,1,0:T(8,128)S(1)}, f32[15,8,128]{2,1,0:T(8,128)}, u32[]{:S(2)}) copy-start(f32[15,8,128]{2,1,0:T(8,128)} %mix_ref.1) | copy-start | bytes 184324
  15.9 7.0 %copy-start.1 = (s32[1,8192]{1,0:T(1,128)S(1)}, s32[1,8192]{1,0:T(1,128)}, u32[]{:S(2)}) copy-start(s32[1,8192]{1,0:T(1,128)} %param.23) | copy-start | bytes 98308
  15.9 7.0 %copy-start.3 = (s32[1,2048]{1,0:T(1,128)S(1)}, s32[1,2048]{1,0:T(1,128)}, u32[]{:S(2)}) copy-start(s32[1,2048]{1,0:T(1,128)} %param.20) | copy-start | bytes 24580
  15.9 7.0 %copy-start.4 = (s32[1,2048]{1,0:T(1,128)S(1)}, s32[1,2048]{1,0:T(1,128)}, u32[]{:S(2)}) copy-start(s32[1,2048]{1,0:T(1,128)} %param.21) | copy-start | bytes 24580
  15.9 7.0 %copy-start.2 = (s32[1,2048]{1,0:T(1,128)S(1)}, s32[1,2048]{1,0:T(1,128)}, u32[]{:S(2)}) copy-start(s32[1,2048]{1,0:T(1,128)} %param.19) | copy-start | bytes 24580
  15.9 10.0 %collective-permute-start.2 = (f32[36,8,128]{2,1,0:T(8,128)S(1)}, f32[36,8,128]{2,1,0:T(8,128)S(1)}, u32[]{:S(2)}, u32[]{:S(2)}) collective-permute-start(f32[36,8,128]{2,1,0:T(8,128)S(1)} %get-tuple-element.29), channel_id=1, source_target_pairs={{1,2},{2,1},{3,4},{4,3},{5,6},{6,5},{7,8},{8,7},{9,10},{10,9},{11,... | collective-permute-start | bytes 442376 | tf_op jit(solution)/shard_map/ppermute | solution.py:396
  20.9 7.5 %collective-permute-start.3 = (f32[36,8,128]{2,1,0:T(8,128)S(1)}, f32[36,8,128]{2,1,0:T(8,128)S(1)}, u32[]{:S(2)}, u32[]{:S(2)}) collective-permute-start(f32[36,8,128]{2,1,0:T(8,128)S(1)} %get-tuple-element.30), channel_id=1, source_target_pairs={{0,1},{1,0},{2,3},{3,2},{4,5},{5,4},{6,7},{7,6},{8,9},{9,8},{10,11... | collective-permute-start | bytes 442376 | tf_op jit(solution)/shard_map/ppermute | solution.py:396
  22.9 0.7 %copy-start.5 = (f32[64]{0:T(128)S(1)}, f32[64]{0:T(128)}, u32[]{:S(2)}) copy-start(f32[64]{0:T(128)} %param.22) | copy-start | bytes 772

commit v4 on v3

--- a/solution.py
+++ b/solution.py
@@ -28,31 +28,19 @@
     return (((iota((ROWS, LANES), 0) >> 2) + parity) & 1) == 0
 
 
-def pack_kernel(*refs):
-    sources, col_ref, held, sem = refs[:6], refs[6], refs[7:13], refs[13]
+def strips(planes):
+    slot = iota((ROWS, LANES), 1) >> 3
+    strip = jnp.zeros((ROWS, LANES), F32)
+    for k, plane in enumerate(planes):
+        strip = jnp.where(slot == k, pltpu.roll(plane, (8 * k + 4) % LANES, 1), strip)
+    return strip
+
+
+def rows_kernel(*refs):
+    sources, (one_ref, two_ref), held, sem = refs[:6], refs[6:8], refs[8:14], refs[14]
     copies = [pltpu.make_async_copy(x, y, sem.at[i]) for i, (x, y) in enumerate(zip(sources, held))]
     for copy in copies:
         copy.start()
-    slot = iota((ROWS, LANES), 1) >> 3
-    for a in range(4):
-        copies[a].wait()
-        strip = jnp.zeros((ROWS, LANES), F32)
-        for k in range(LEVELS):
-            strip = jnp.where(slot == k, pltpu.roll(held[a][k], (8 * k + 4) % LANES, 1), strip)
-        col_ref[a] = strip
-    copies[4].wait()
-    copies[5].wait()
-    strip = jnp.where(slot == 0, pltpu.roll(held[4][...], 4, 1), jnp.zeros((ROWS, LANES), F32))
-    col_ref[4] = jnp.where(slot == 1, pltpu.roll(held[5][...].astype(F32), 12, 1), strip)
-
-
-def side_columns(first_ref, second_ref):
-    parity = lax.axis_index("gx") & 1
-    mask = (((iota((ROWS, LANES), 1) >> 2) + parity) & 1) == 0
-    return [jnp.where(mask, second_ref[a], first_ref[a]) for a in range(5)]
-
-
-def rows_kernel(t_ref, s_ref, u_ref, v_ref, kap_ref, dep_ref, second_ref, first_ref, one_ref, two_ref):
     mask = row_mask(lax.axis_index("gy") & 1)
 
     def put(i, here, there):
@@ -60,20 +48,43 @@
         one_ref[i] = jnp.where(mask, there, here)
         two_ref[i] = jnp.where(mask, here, there)
 
+    for a in range(4):
+        copies[a].wait()
+        for k in range(8):
+            put(a * 8 + k, held[a][k], held[a][k + 8])
+    copies[4].wait()
+    copies[5].wait()
+    put(32, held[4][...], held[5][...].astype(F32))
+
+
+def unpair(i, mask, one_ref, two_ref):
+    x, y = one_ref[i], two_ref[i]
+    return jnp.where(mask, x, y), pltpu.roll(jnp.where(mask, y, x), 4, 0)
+
+
+def columns_kernel(local_ref, two_ref, one_ref, col_ref):
+    mask = row_mask(lax.axis_index("gy") & 1)
+    for a in range(4):
+        pairs = [unpair(a * 8 + k, mask, one_ref, two_ref) for k in range(8)]
+        col_ref[a] = local_ref[a]
+        col_ref[5 + a] = strips([x[0] for x in pairs] + [x[1] for x in pairs])
+    col_ref[4] = local_ref[4]
+    col_ref[9] = strips(unpair(32, mask, one_ref, two_ref))
+
+
+def side_columns(first_ref, second_ref):
+    parity = lax.axis_index("gx") & 1
+    mask = (((iota((ROWS, LANES), 1) >> 2) + parity) & 1) == 0
+    return [jnp.where(mask, second_ref[a], first_ref[a]) for a in range(10)]
+
+
+def prep_kernel(
+    src_ref, sky_ref, ptr_ref, area_ref, place_ref, mix_ref, t_ref, s_ref, u_ref, v_ref, kap_ref, dep_ref,
+    inv_ref, down_ref, up_ref, weight_ref, owner_ref, rank_ref, slot_ref, col_ref,
+):
     for a, ref in enumerate((t_ref, s_ref, u_ref, v_ref)):
-        for k in range(8):
-            put(a * 8 + k, ref[k], ref[k + 8])
-    put(32, kap_ref[...], dep_ref[...].astype(F32))
-    side = side_columns(first_ref, second_ref)
-    side.append(jnp.zeros((ROWS, LANES), F32))
-    for i in range(3):
-        put(33 + i, side[2 * i], side[2 * i + 1])
-
-
-def prep_kernel(
-    src_ref, sky_ref, ptr_ref, area_ref, place_ref, mix_ref, dep_ref,
-    inv_ref, down_ref, up_ref, weight_ref, owner_ref, rank_ref, slot_ref,
-):
+        col_ref[a] = strips([ref[k] for k in range(LEVELS)])
+    col_ref[4] = strips([kap_ref[...], dep_ref[...].astype(F32)])
     q = lax.axis_index("gx")
     dep = dep_ref[...]
     above = jnp.zeros((ROWS, LANES), F32)
@@ -169,7 +180,7 @@
 
 
 def main_kernel(
-    t_ref, s_ref, u_ref, v_ref, kap_ref, dep_ref, second_ref, first_ref, two_ref, one_ref,
+    t_ref, s_ref, u_ref, v_ref, kap_ref, dep_ref, first_ref, second_ref, two_ref, one_ref,
     inv_ref, down_ref, up_ref, weight_ref, owner_ref, rank_ref, slot_ref,
     tout_ref, sout_ref, send_ref, strip_ref, face_ref,
 ):
@@ -204,14 +215,10 @@
         return a, b, h, g
 
     def pair(i):
-        x, y = one_ref[i], two_ref[i]
-        return jnp.where(mask, x, y), pltpu.roll(jnp.where(mask, y, x), 4, 0)
+        return unpair(i, mask, one_ref, two_ref)
 
     side = side_columns(first_ref, second_ref)
-    corner = []
-    for i in range(3):
-        corner.extend(pair(33 + i))
-
+    corner = side[5:]
     for i in range(5):
         strip_ref[0, i] = side[i]
         strip_ref[1, i] = corner[i]
@@ -377,11 +384,10 @@
         flooded_strata,
     )
     plane = (ROWS, LANES)
-    strips = ((36,) + plane, F32)
-    column, *held = call(
-        pack_kernel,
-        "pack",
-        [((5,) + plane, F32)] + [(x.shape, x.dtype) for x in fields],
+    one, two, *held = call(
+        rows_kernel,
+        "rows",
+        [((33,) + plane, F32)] * 2 + [(x.shape, x.dtype) for x in fields],
         6,
         1 << 18,
         in_specs=[pl.BlockSpec(memory_space=pltpu.HBM)] * 6,
@@ -395,13 +401,10 @@
                 pairs += [(i, (i + 1) % count), ((i + 1) % count, i)]
         return lax.ppermute(x, axis, pairs)
 
-    second = swap(column, "gx", nx, 1, True)
-    first = swap(column, "gx", nx, 0, True)
-    one, two = call(rows_kernel, "rows", [strips, strips], 8, 1 << 16)(*held, second, first)
     two = swap(two, "gy", ny, 1, False)
     one = swap(one, "gy", ny, 0, False)
     column3 = ((LEVELS,) + plane, F32)
-    prepared = call(
+    *prepared, column = call(
         prep_kernel,
         "prep",
         [
@@ -412,8 +415,9 @@
             ((32, 5 * LANES), BF16),
             ((4,) + plane, F32),
             ((32, LANES), F32),
+            ((5,) + plane, F32),
         ],
-        7,
+        12,
         1 << 26,
     )(
         patch_sea_source.reshape(16, LANES),
@@ -422,8 +426,11 @@
         patch_measures.reshape(1, 64),
         holder_ordering.reshape(64, LANES),
         stratum_interface_mixing,
-        held[5],
-    )
+        *held,
+    )
+    (column,) = call(columns_kernel, "columns", [((10,) + plane, F32)], 3, 1 << 16)(column, two, one)
+    second = swap(column, "gx", nx, 1, True)
+    first = swap(column, "gx", nx, 0, True)
     temperature, salinity, send = call(
         main_kernel,
         "main",
@@ -431,7 +438,7 @@
         17,
         1 << 24,
         scratch_shapes=[pltpu.VMEM((2, 5) + plane, F32), pltpu.VMEM((4, 4) + plane, F32)],
-    )(*held, second, first, two, one, *prepared)
+    )(*held, first, second, two, one, *prepared)
     order = [[(i + LEAD) % nx for i in range(nx)]]
     got = lax.all_to_all(send.reshape(nx, 1, LANES), "gx", 0, 0, tiled=True, axis_index_groups=order)
     (air,) = call(owner_kernel, "owner", [((2, 1, 256), F32)], 1, 1 << 20)(got.reshape(nx, LANES))

time: 47.3 us -> 45.4 us (0.960)
  starting transfers between devices: 19.7 us -> 18.1 us
  waiting for transfers between devices: 5.51 us -> 4.9 us
    ppermute x4, starting transfers between devices: 19.7 us -> 18.1 us  [swap(): return lax.ppermute(x, axis, pairs)]
    ppermute x4, waiting for transfers between devices: 5.51 us -> 4.9 us  [swap(): return lax.ppermute(x, axis, pairs)]
where the time goes in v4:
time: 45.4 us; the launch traced here: 45.1 us
  starting transfers between devices  18.1 us (40%)
  blocking collectives  14.8 us (33%)
  Pallas kernels  5.8 us (13%)
  waiting for transfers between devices  4.9 us (11%)
  between operations  0.76 us (2%)
  local copies, waits for them, and re-layouts  0.68 us (1%)
    ppermute x4, starting transfers between devices, swap(): return lax.ppermute(x, axis, pairs)  18.1 us
    all_to_all x1, blocking collectives, shards(): lax.all_to_all(send.reshape(nx, 1, LANES), 'gx', 0, 0, tiled=True, axis_i...  14.8 us
    ppermute x4, waiting for transfers between devices, swap(): return lax.ppermute(x, axis, pairs)  4.9 us
    pallas_call x1, Pallas kernels, shards(): call(main_kernel, 'main', [column3, column3, ((32, LANES), F32)], 17, 1 <...  3.23 us
    pallas_call x1, Pallas kernels, shards(): call(rows_kernel, 'rows', [((33,) + plane, F32)] * 2 + [(x.shape, x.dtype...  1.03 us
  transfers between devices with their start and end apart: 4, of which 3 were waited for; matrix products, arithmetic and copies ran while one was open for 0% of the time, Pallas kernels for 1%

profile of v4, /device:TPU:24, one launch (start us, length us, event | category | flops | bytes accessed | tf_op | source)
XLA Modules:
  0.0 45.1 jit_solution(12226089154343275932)
XLA Ops:
  0.6 0.0 copy-start
  0.6 0.0 copy-start.1
  0.7 0.0 copy-start.4
  0.7 1.0 %rows.1 = (f32[33,8,128]{2,1,0:T(8,128)S(1)}, f32[33,8,128]{2,1,0:T(8,128)S(1)}, f32[16,8,128]{2,1,0:T(8,128)S(1)}, f32[16,8,128]{2,1,0:T(8,128)S(1)}, f32[16,8,...) custom-call(f32[16,8,128]{2,1,0:T(8,128)} %refs_0_.1, ...), custom_call_target="tpu_custom_call" | custom-call | flops 262144 | bytes 1048576 | tf_op jit(solution)/shard_map/rows/pallas_call | solution.py:387
  1.7 4.8 %collective-permute-start = (f32[33,8,128]{2,1,0:T(8,128)S(1)}, f32[33,8,128]{2,1,0:T(8,128)S(1)}, u32[]{:S(2)}, u32[]{:S(2)}) collective-permute-start(f32[33,8,128]{2,1,0:T(8,128)S(1)} %get-tuple-element.29), channel_id=1, source_target_pairs={{1,2},{2,1},{3,4},{4,3},{5,6},{6,5},{7,8},{8,7},{9,10},{10,9},{11,... | collective-permute-start | bytes 405512 | tf_op jit(solution)/shard_map/ppermute | solution.py:402
  6.6 2.0 %collective-permute-start.1 = (f32[33,8,128]{2,1,0:T(8,128)S(1)}, f32[33,8,128]{2,1,0:T(8,128)S(1)}, u32[]{:S(2)}, u32[]{:S(2)}) collective-permute-start(f32[33,8,128]{2,1,0:T(8,128)S(1)} %get-tuple-element.30), channel_id=1, source_target_pairs={{0,1},{1,0},{2,3},{3,2},{4,5},{5,4},{6,7},{7,6},{8,9},{9,8},{10,11... | collective-permute-start | bytes 405512 | tf_op jit(solution)/shard_map/ppermute | solution.py:402
  8.5 0.0 copy-start.3
  8.5 0.0 copy-start.2
  8.5 0.0 copy-start.5
  8.6 0.0 copy-done
  8.6 0.0 copy-done.1
  8.6 0.0 copy-done.4
  8.6 0.6 %copy-done.3 = s32[1,2048]{1,0:T(1,128)S(1)} copy-done((s32[1,2048]{1,0:T(1,128)S(1)}, s32[1,2048]{1,0:T(1,128)}, u32[]{:S(2)}) %copy-start.3) | copy-done | bytes 8216
  9.2 0.0 copy-done.2
  9.2 0.0 copy-done.5
  9.2 0.5 %prep.1 = (f32[16,8,128]{2,1,0:T(8,128)S(1)}, f32[16,8,128]{2,1,0:T(8,128)S(1)}, f32[16,8,128]{2,1,0:T(8,128)S(1)}, f32[4,8,128]{2,1,0:T(8,128)S(1)}, bf16[32,64...) custom-call(s32[16,128]{1,0:T(8,128)S(1)} %bitcast.12, ...), custom_call_target="tpu_custom_call" | custom-call | flops 67108864 | bytes 1048576 | tf_op jit(solution)/shard_map/prep/pallas_call | solution.py:407
  9.8 1.3 %collective-permute-done.two_ref = f32[33,8,128]{2,1,0:T(8,128)S(1)} collective-permute-done((f32[33,8,128]{2,1,0:T(8,128)S(1)}, f32[33,8,128]{2,1,0:T(8,128)S(1)}, u32[]{:S(2)}, u32[]{:S(2)}) %collective-permute-start) | collective-permute-done | bytes 135200 | tf_op jit(solution)/shard_map/ppermute | solution.py:402
  11.0 2.5 %collective-permute-done.1.one_ref = f32[33,8,128]{2,1,0:T(8,128)S(1)} collective-permute-done((f32[33,8,128]{2,1,0:T(8,128)S(1)}, f32[33,8,128]{2,1,0:T(8,128)S(1)}, u32[]{:S(2)}, u32[]{:S(2)}) %collective-permute-start.1) | collective-permute-done | bytes 135200 | tf_op jit(solution)/shard_map/ppermute | solution.py:402
  13.5 0.1 columns.1
  13.6 9.4 %collective-permute-start.3 = (f32[10,8,128]{2,1,0:T(8,128)S(1)}, f32[10,8,128]{2,1,0:T(8,128)S(1)}, u32[]{:S(2)}, u32[]{:S(2)}) collective-permute-start(f32[10,8,128]{2,1,0:T(8,128)S(1)} %columns.1), channel_id=1, source_target_pairs={{16,32},{32,16},{48,64},{64,48},{80,96},{96,80},{112,128},{128,112... | collective-permute-start | bytes 122888 | tf_op jit(solution)/shard_map/ppermute | solution.py:402
  23.0 1.9 %collective-permute-start.2 = (f32[10,8,128]{2,1,0:T(8,128)S(1)}, f32[10,8,128]{2,1,0:T(8,128)S(1)}, u32[]{:S(2)}, u32[]{:S(2)}) collective-permute-start(f32[10,8,128]{2,1,0:T(8,128)S(1)} %columns.1), channel_id=1, source_target_pairs={{0,16},{16,0},{32,48},{48,32},{64,80},{80,64},{96,112},{112,96},{1... | collective-permute-start | bytes 122888 | tf_op jit(solution)/shard_map/ppermute | solution.py:402
  25.0 0.0 collective-permute-done.3.second_ref
  25.0 1.2 %collective-permute-done.2.first_ref = f32[10,8,128]{2,1,0:T(8,128)S(1)} collective-permute-done((f32[10,8,128]{2,1,0:T(8,128)S(1)}, f32[10,8,128]{2,1,0:T(8,128)S(1)}, u32[]{:S(2)}, u32[]{:S(2)}) %collective-permute-start.2) | collective-permute-done | bytes 40992 | tf_op jit(solution)/shard_map/ppermute | solution.py:402
  26.1 3.2 %main.1 = (f32[16,8,128]{2,1,0:T(8,128)}, f32[16,8,128]{2,1,0:T(8,128)}, f32[32,128]{1,0:T(8,128)S(1)}) custom-call(f32[16,8,128]{2,1,0:T(8,128)S(1)} %get-tuple-element.22.t_ref, f32[16,8,128]{2,1,0:T(8,128)S(1)} %get-tuple-element.23.s_ref, f32[16,8,128]{2,1,0:T(8,128)S(1)} %get-tuple-element.24.u_ref, f32[16,8,128]{2,1,0:T(8,128)S(1)} %get-tuple-element.25.v_ref, ...), custom_call_target="tpu_custom_call" | custom-call | flops 16777216 | bytes 1048576 | tf_op jit(solution)/shard_map/main/pallas_call | solution.py:434
  29.4 14.8 %all_to_all.5 = f32[32,1,128]{2,1,0:T(1,128)S(1)} all-to-all(f32[32,1,128]{2,1,0:T(1,128)S(1)} %bitcast.11), channel_id=1, replica_groups={{320,336,352,368,384,400,416,432,448,464,480,496,0,16,32,48,64,80,96,11..., dimensions={0} | all-to-all | bytes 32768 | tf_op jit(solution)/shard_map/all_to_all | solution.py:443
  44.2 0.9 %owner.1 = f32[2,1,256]{2,1,0:T(1,128)} custom-call(f32[32,128]{1,0:T(8,128)S(1)} %bitcast.9), custom_call_target="tpu_custom_call" | custom-call | flops 1048576 | bytes 1048576 | tf_op jit(solution)/shard_map/owner/pallas_call | solution.py:444
Async XLA Ops:
  0.6 7.9 %copy-start = (f32[15,8,128]{2,1,0:T(8,128)S(1)}, f32[15,8,128]{2,1,0:T(8,128)}, u32[]{:S(2)}) copy-start(f32[15,8,128]{2,1,0:T(8,128)} %mix_ref.1) | copy-start | bytes 184324
  0.6 7.9 %copy-start.1 = (s32[1,8192]{1,0:T(1,128)S(1)}, s32[1,8192]{1,0:T(1,128)}, u32[]{:S(2)}) copy-start(s32[1,8192]{1,0:T(1,128)} %param.23) | copy-start | bytes 98308
  0.7 7.9 %copy-start.4 = (s32[1,2048]{1,0:T(1,128)S(1)}, s32[1,2048]{1,0:T(1,128)}, u32[]{:S(2)}) copy-start(s32[1,2048]{1,0:T(1,128)} %param.21) | copy-start | bytes 24580
  1.7 9.3 %collective-permute-start = (f32[33,8,128]{2,1,0:T(8,128)S(1)}, f32[33,8,128]{2,1,0:T(8,128)S(1)}, u32[]{:S(2)}, u32[]{:S(2)}) collective-permute-start(f32[33,8,128]{2,1,0:T(8,128)S(1)} %get-tuple-element.29), channel_id=1, source_target_pairs={{1,2},{2,1},{3,4},{4,3},{5,6},{6,5},{7,8},{8,7},{9,10},{10,9},{11,... | collective-permute-start | bytes 405512 | tf_op jit(solution)/shard_map/ppermute | solution.py:402
  6.6 6.9 %collective-permute-start.1 = (f32[33,8,128]{2,1,0:T(8,128)S(1)}, f32[33,8,128]{2,1,0:T(8,128)S(1)}, u32[]{:S(2)}, u32[]{:S(2)}) collective-permute-start(f32[33,8,128]{2,1,0:T(8,128)S(1)} %get-tuple-element.30), channel_id=1, source_target_pairs={{0,1},{1,0},{2,3},{3,2},{4,5},{5,4},{6,7},{7,6},{8,9},{9,8},{10,11... | collective-permute-start | bytes 405512 | tf_op jit(solution)/shard_map/ppermute | solution.py:402
  8.5 0.7 %copy-start.3 = (s32[1,2048]{1,0:T(1,128)S(1)}, s32[1,2048]{1,0:T(1,128)}, u32[]{:S(2)}) copy-start(s32[1,2048]{1,0:T(1,128)} %param.20) | copy-start | bytes 24580
  8.5 0.7 %copy-start.2 = (s32[1,2048]{1,0:T(1,128)S(1)}, s32[1,2048]{1,0:T(1,128)}, u32[]{:S(2)}) copy-start(s32[1,2048]{1,0:T(1,128)} %param.19) | copy-start | bytes 24580
  8.5 0.7 %copy-start.5 = (f32[64]{0:T(128)S(1)}, f32[64]{0:T(128)}, u32[]{:S(2)}) copy-start(f32[64]{0:T(128)} %param.22) | copy-start | bytes 772
  13.6 11.3 %collective-permute-start.3 = (f32[10,8,128]{2,1,0:T(8,128)S(1)}, f32[10,8,128]{2,1,0:T(8,128)S(1)}, u32[]{:S(2)}, u32[]{:S(2)}) collective-permute-start(f32[10,8,128]{2,1,0:T(8,128)S(1)} %columns.1), channel_id=1, source_target_pairs={{16,32},{32,16},{48,64},{64,48},{80,96},{96,80},{112,128},{128,112... | collective-permute-start | bytes 122888 | tf_op jit(solution)/shard_map/ppermute | solution.py:402
  23.0 3.1 %collective-permute-start.2 = (f32[10,8,128]{2,1,0:T(8,128)S(1)}, f32[10,8,128]{2,1,0:T(8,128)S(1)}, u32[]{:S(2)}, u32[]{:S(2)}) collective-permute-start(f32[10,8,128]{2,1,0:T(8,128)S(1)} %columns.1), channel_id=1, source_target_pairs={{0,16},{16,0},{32,48},{48,32},{64,80},{80,64},{96,112},{112,96},{1... | collective-permute-start | bytes 122888 | tf_op jit(solution)/shard_map/ppermute | solution.py:402

commit v5 on v4

--- a/solution.py
+++ b/solution.py
@@ -13,7 +13,7 @@
 BF16 = jnp.bfloat16
 
 
-LEAD = 20
+LEAD = 18
 
 
 def seat(place):

time: 45.4 us -> 45 us (level)
  no operation moved by 1% of the time
where the time goes in v5:
time: 45 us; the launch traced here: 44.7 us
  starting transfers between devices  18.1 us (40%)
  blocking collectives  14.5 us (32%)
  Pallas kernels  5.8 us (13%)
  waiting for transfers between devices  4.9 us (11%)
  between operations  0.76 us (2%)
  local copies, waits for them, and re-layouts  0.68 us (2%)
    ppermute x4, starting transfers between devices, swap(): return lax.ppermute(x, axis, pairs)  18.1 us
    all_to_all x1, blocking collectives, shards(): lax.all_to_all(send.reshape(nx, 1, LANES), 'gx', 0, 0, tiled=True, axis_i...  14.5 us
    ppermute x4, waiting for transfers between devices, swap(): return lax.ppermute(x, axis, pairs)  4.9 us
    pallas_call x1, Pallas kernels, shards(): call(main_kernel, 'main', [column3, column3, ((32, LANES), F32)], 17, 1 <...  3.23 us
    pallas_call x1, Pallas kernels, shards(): call(rows_kernel, 'rows', [((33,) + plane, F32)] * 2 + [(x.shape, x.dtype...  1.03 us
  transfers between devices with their start and end apart: 4, of which 3 were waited for; matrix products, arithmetic and copies ran while one was open for 0% of the time, Pallas kernels for 1%

profile of v5, /device:TPU:24, one launch (start us, length us, event | category | flops | bytes accessed | tf_op | source)
XLA Modules:
  0.0 44.7 jit_solution(13726205971113618130)
XLA Ops:
  0.6 0.0 copy-start
  0.6 0.0 copy-start.1
  0.7 0.0 copy-start.4
  0.7 1.0 %rows.1 = (f32[33,8,128]{2,1,0:T(8,128)S(1)}, f32[33,8,128]{2,1,0:T(8,128)S(1)}, f32[16,8,128]{2,1,0:T(8,128)S(1)}, f32[16,8,128]{2,1,0:T(8,128)S(1)}, f32[16,8,...) custom-call(f32[16,8,128]{2,1,0:T(8,128)} %refs_0_.1, ...), custom_call_target="tpu_custom_call" | custom-call | flops 262144 | bytes 1048576 | tf_op jit(solution)/shard_map/rows/pallas_call | solution.py:387
  1.7 4.8 %collective-permute-start = (f32[33,8,128]{2,1,0:T(8,128)S(1)}, f32[33,8,128]{2,1,0:T(8,128)S(1)}, u32[]{:S(2)}, u32[]{:S(2)}) collective-permute-start(f32[33,8,128]{2,1,0:T(8,128)S(1)} %get-tuple-element.29), channel_id=1, source_target_pairs={{1,2},{2,1},{3,4},{4,3},{5,6},{6,5},{7,8},{8,7},{9,10},{10,9},{11,... | collective-permute-start | bytes 405512 | tf_op jit(solution)/shard_map/ppermute | solution.py:402
  6.6 2.0 %collective-permute-start.1 = (f32[33,8,128]{2,1,0:T(8,128)S(1)}, f32[33,8,128]{2,1,0:T(8,128)S(1)}, u32[]{:S(2)}, u32[]{:S(2)}) collective-permute-start(f32[33,8,128]{2,1,0:T(8,128)S(1)} %get-tuple-element.30), channel_id=1, source_target_pairs={{0,1},{1,0},{2,3},{3,2},{4,5},{5,4},{6,7},{7,6},{8,9},{9,8},{10,11... | collective-permute-start | bytes 405512 | tf_op jit(solution)/shard_map/ppermute | solution.py:402
  8.5 0.0 copy-start.3
  8.5 0.0 copy-start.2
  8.5 0.0 copy-start.5
  8.6 0.0 copy-done
  8.6 0.0 copy-done.1
  8.6 0.0 copy-done.4
  8.6 0.6 %copy-done.3 = s32[1,2048]{1,0:T(1,128)S(1)} copy-done((s32[1,2048]{1,0:T(1,128)S(1)}, s32[1,2048]{1,0:T(1,128)}, u32[]{:S(2)}) %copy-start.3) | copy-done | bytes 8216
  9.2 0.0 copy-done.2
  9.2 0.0 copy-done.5
  9.2 0.5 %prep.1 = (f32[16,8,128]{2,1,0:T(8,128)S(1)}, f32[16,8,128]{2,1,0:T(8,128)S(1)}, f32[16,8,128]{2,1,0:T(8,128)S(1)}, f32[4,8,128]{2,1,0:T(8,128)S(1)}, bf16[32,64...) custom-call(s32[16,128]{1,0:T(8,128)S(1)} %bitcast.12, ...), custom_call_target="tpu_custom_call" | custom-call | flops 67108864 | bytes 1048576 | tf_op jit(solution)/shard_map/prep/pallas_call | solution.py:407
  9.8 1.3 %collective-permute-done.two_ref = f32[33,8,128]{2,1,0:T(8,128)S(1)} collective-permute-done((f32[33,8,128]{2,1,0:T(8,128)S(1)}, f32[33,8,128]{2,1,0:T(8,128)S(1)}, u32[]{:S(2)}, u32[]{:S(2)}) %collective-permute-start) | collective-permute-done | bytes 135200 | tf_op jit(solution)/shard_map/ppermute | solution.py:402
  11.0 2.5 %collective-permute-done.1.one_ref = f32[33,8,128]{2,1,0:T(8,128)S(1)} collective-permute-done((f32[33,8,128]{2,1,0:T(8,128)S(1)}, f32[33,8,128]{2,1,0:T(8,128)S(1)}, u32[]{:S(2)}, u32[]{:S(2)}) %collective-permute-start.1) | collective-permute-done | bytes 135200 | tf_op jit(solution)/shard_map/ppermute | solution.py:402
  13.5 0.1 columns.1
  13.6 9.4 %collective-permute-start.3 = (f32[10,8,128]{2,1,0:T(8,128)S(1)}, f32[10,8,128]{2,1,0:T(8,128)S(1)}, u32[]{:S(2)}, u32[]{:S(2)}) collective-permute-start(f32[10,8,128]{2,1,0:T(8,128)S(1)} %columns.1), channel_id=1, source_target_pairs={{16,32},{32,16},{48,64},{64,48},{80,96},{96,80},{112,128},{128,112... | collective-permute-start | bytes 122888 | tf_op jit(solution)/shard_map/ppermute | solution.py:402
  23.0 1.9 %collective-permute-start.2 = (f32[10,8,128]{2,1,0:T(8,128)S(1)}, f32[10,8,128]{2,1,0:T(8,128)S(1)}, u32[]{:S(2)}, u32[]{:S(2)}) collective-permute-start(f32[10,8,128]{2,1,0:T(8,128)S(1)} %columns.1), channel_id=1, source_target_pairs={{0,16},{16,0},{32,48},{48,32},{64,80},{80,64},{96,112},{112,96},{1... | collective-permute-start | bytes 122888 | tf_op jit(solution)/shard_map/ppermute | solution.py:402
  25.0 0.0 collective-permute-done.3.second_ref
  25.0 1.2 %collective-permute-done.2.first_ref = f32[10,8,128]{2,1,0:T(8,128)S(1)} collective-permute-done((f32[10,8,128]{2,1,0:T(8,128)S(1)}, f32[10,8,128]{2,1,0:T(8,128)S(1)}, u32[]{:S(2)}, u32[]{:S(2)}) %collective-permute-start.2) | collective-permute-done | bytes 40992 | tf_op jit(solution)/shard_map/ppermute | solution.py:402
  26.1 3.2 %main.1 = (f32[16,8,128]{2,1,0:T(8,128)}, f32[16,8,128]{2,1,0:T(8,128)}, f32[32,128]{1,0:T(8,128)S(1)}) custom-call(f32[16,8,128]{2,1,0:T(8,128)S(1)} %get-tuple-element.22.t_ref, f32[16,8,128]{2,1,0:T(8,128)S(1)} %get-tuple-element.23.s_ref, f32[16,8,128]{2,1,0:T(8,128)S(1)} %get-tuple-element.24.u_ref, f32[16,8,128]{2,1,0:T(8,128)S(1)} %get-tuple-element.25.v_ref, ...), custom_call_target="tpu_custom_call" | custom-call | flops 16777216 | bytes 1048576 | tf_op jit(solution)/shard_map/main/pallas_call | solution.py:434
  29.4 14.5 %all_to_all.5 = f32[32,1,128]{2,1,0:T(1,128)S(1)} all-to-all(f32[32,1,128]{2,1,0:T(1,128)S(1)} %bitcast.11), channel_id=1, replica_groups={{288,304,320,336,352,368,384,400,416,432,448,464,480,496,0,16,32,48,64,..., dimensions={0} | all-to-all | bytes 32768 | tf_op jit(solution)/shard_map/all_to_all | solution.py:443
  43.8 0.9 %owner.1 = f32[2,1,256]{2,1,0:T(1,128)} custom-call(f32[32,128]{1,0:T(8,128)S(1)} %bitcast.9), custom_call_target="tpu_custom_call" | custom-call | flops 1048576 | bytes 1048576 | tf_op jit(solution)/shard_map/owner/pallas_call | solution.py:444
Async XLA Ops:
  0.6 7.9 %copy-start = (f32[15,8,128]{2,1,0:T(8,128)S(1)}, f32[15,8,128]{2,1,0:T(8,128)}, u32[]{:S(2)}) copy-start(f32[15,8,128]{2,1,0:T(8,128)} %mix_ref.1) | copy-start | bytes 184324
  0.6 7.9 %copy-start.1 = (s32[1,8192]{1,0:T(1,128)S(1)}, s32[1,8192]{1,0:T(1,128)}, u32[]{:S(2)}) copy-start(s32[1,8192]{1,0:T(1,128)} %param.23) | copy-start | bytes 98308
  0.7 7.9 %copy-start.4 = (s32[1,2048]{1,0:T(1,128)S(1)}, s32[1,2048]{1,0:T(1,128)}, u32[]{:S(2)}) copy-start(s32[1,2048]{1,0:T(1,128)} %param.21) | copy-start | bytes 24580
  1.7 9.3 %collective-permute-start = (f32[33,8,128]{2,1,0:T(8,128)S(1)}, f32[33,8,128]{2,1,0:T(8,128)S(1)}, u32[]{:S(2)}, u32[]{:S(2)}) collective-permute-start(f32[33,8,128]{2,1,0:T(8,128)S(1)} %get-tuple-element.29), channel_id=1, source_target_pairs={{1,2},{2,1},{3,4},{4,3},{5,6},{6,5},{7,8},{8,7},{9,10},{10,9},{11,... | collective-permute-start | bytes 405512 | tf_op jit(solution)/shard_map/ppermute | solution.py:402
  6.6 6.9 %collective-permute-start.1 = (f32[33,8,128]{2,1,0:T(8,128)S(1)}, f32[33,8,128]{2,1,0:T(8,128)S(1)}, u32[]{:S(2)}, u32[]{:S(2)}) collective-permute-start(f32[33,8,128]{2,1,0:T(8,128)S(1)} %get-tuple-element.30), channel_id=1, source_target_pairs={{0,1},{1,0},{2,3},{3,2},{4,5},{5,4},{6,7},{7,6},{8,9},{9,8},{10,11... | collective-permute-start | bytes 405512 | tf_op jit(solution)/shard_map/ppermute | solution.py:402
  8.5 0.7 %copy-start.3 = (s32[1,2048]{1,0:T(1,128)S(1)}, s32[1,2048]{1,0:T(1,128)}, u32[]{:S(2)}) copy-start(s32[1,2048]{1,0:T(1,128)} %param.20) | copy-start | bytes 24580
  8.5 0.7 %copy-start.2 = (s32[1,2048]{1,0:T(1,128)S(1)}, s32[1,2048]{1,0:T(1,128)}, u32[]{:S(2)}) copy-start(s32[1,2048]{1,0:T(1,128)} %param.19) | copy-start | bytes 24580
  8.5 0.7 %copy-start.5 = (f32[64]{0:T(128)S(1)}, f32[64]{0:T(128)}, u32[]{:S(2)}) copy-start(f32[64]{0:T(128)} %param.22) | copy-start | bytes 772
  13.6 11.3 %collective-permute-start.3 = (f32[10,8,128]{2,1,0:T(8,128)S(1)}, f32[10,8,128]{2,1,0:T(8,128)S(1)}, u32[]{:S(2)}, u32[]{:S(2)}) collective-permute-start(f32[10,8,128]{2,1,0:T(8,128)S(1)} %columns.1), channel_id=1, source_target_pairs={{16,32},{32,16},{48,64},{64,48},{80,96},{96,80},{112,128},{128,112... | collective-permute-start | bytes 122888 | tf_op jit(solution)/shard_map/ppermute | solution.py:402
  23.0 3.1 %collective-permute-start.2 = (f32[10,8,128]{2,1,0:T(8,128)S(1)}, f32[10,8,128]{2,1,0:T(8,128)S(1)}, u32[]{:S(2)}, u32[]{:S(2)}) collective-permute-start(f32[10,8,128]{2,1,0:T(8,128)S(1)} %columns.1), channel_id=1, source_target_pairs={{0,16},{16,0},{32,48},{48,32},{64,80},{80,64},{96,112},{112,96},{1... | collective-permute-start | bytes 122888 | tf_op jit(solution)/shard_map/ppermute | solution.py:402

commit v6 on v5

--- a/solution.py
+++ b/solution.py
@@ -13,7 +13,7 @@
 BF16 = jnp.bfloat16
 
 
-LEAD = 18
+LEAD = 17
 
 
 def seat(place):

time: 45 us -> 44.7 us (level)
  no operation moved by 1% of the time
where the time goes in v6:
time: 44.7 us; the launch traced here: 44.4 us
  starting transfers between devices  18.1 us (40%)
  blocking collectives  14.2 us (32%)
  Pallas kernels  5.8 us (13%)
  waiting for transfers between devices  4.9 us (11%)
  between operations  0.76 us (2%)
  local copies, waits for them, and re-layouts  0.68 us (2%)
    ppermute x4, starting transfers between devices, swap(): return lax.ppermute(x, axis, pairs)  18.1 us
    all_to_all x1, blocking collectives, shards(): lax.all_to_all(send.reshape(nx, 1, LANES), 'gx', 0, 0, tiled=True, axis_i...  14.2 us
    ppermute x4, waiting for transfers between devices, swap(): return lax.ppermute(x, axis, pairs)  4.9 us
    pallas_call x1, Pallas kernels, shards(): call(main_kernel, 'main', [column3, column3, ((32, LANES), F32)], 17, 1 <...  3.23 us
    pallas_call x1, Pallas kernels, shards(): call(rows_kernel, 'rows', [((33,) + plane, F32)] * 2 + [(x.shape, x.dtype...  1.03 us
  transfers between devices with their start and end apart: 4, of which 3 were waited for; matrix products, arithmetic and copies ran while one was open for 0% of the time, Pallas kernels for 1%

profile of v6, /device:TPU:24, one launch (start us, length us, event | category | flops | bytes accessed | tf_op | source)
XLA Modules:
  0.0 44.4 jit_solution(9799744873457145557)
XLA Ops:
  0.6 0.0 copy-start
  0.6 0.0 copy-start.1
  0.7 0.0 copy-start.4
  0.7 1.0 %rows.1 = (f32[33,8,128]{2,1,0:T(8,128)S(1)}, f32[33,8,128]{2,1,0:T(8,128)S(1)}, f32[16,8,128]{2,1,0:T(8,128)S(1)}, f32[16,8,128]{2,1,0:T(8,128)S(1)}, f32[16,8,...) custom-call(f32[16,8,128]{2,1,0:T(8,128)} %refs_0_.1, ...), custom_call_target="tpu_custom_call" | custom-call | flops 262144 | bytes 1048576 | tf_op jit(solution)/shard_map/rows/pallas_call | solution.py:387
  1.7 4.8 %collective-permute-start = (f32[33,8,128]{2,1,0:T(8,128)S(1)}, f32[33,8,128]{2,1,0:T(8,128)S(1)}, u32[]{:S(2)}, u32[]{:S(2)}) collective-permute-start(f32[33,8,128]{2,1,0:T(8,128)S(1)} %get-tuple-element.29), channel_id=1, source_target_pairs={{1,2},{2,1},{3,4},{4,3},{5,6},{6,5},{7,8},{8,7},{9,10},{10,9},{11,... | collective-permute-start | bytes 405512 | tf_op jit(solution)/shard_map/ppermute | solution.py:402
  6.6 2.0 %collective-permute-start.1 = (f32[33,8,128]{2,1,0:T(8,128)S(1)}, f32[33,8,128]{2,1,0:T(8,128)S(1)}, u32[]{:S(2)}, u32[]{:S(2)}) collective-permute-start(f32[33,8,128]{2,1,0:T(8,128)S(1)} %get-tuple-element.30), channel_id=1, source_target_pairs={{0,1},{1,0},{2,3},{3,2},{4,5},{5,4},{6,7},{7,6},{8,9},{9,8},{10,11... | collective-permute-start | bytes 405512 | tf_op jit(solution)/shard_map/ppermute | solution.py:402
  8.5 0.0 copy-start.3
  8.5 0.0 copy-start.2
  8.5 0.0 copy-start.5
  8.6 0.0 copy-done
  8.6 0.0 copy-done.1
  8.6 0.0 copy-done.4
  8.6 0.6 %copy-done.3 = s32[1,2048]{1,0:T(1,128)S(1)} copy-done((s32[1,2048]{1,0:T(1,128)S(1)}, s32[1,2048]{1,0:T(1,128)}, u32[]{:S(2)}) %copy-start.3) | copy-done | bytes 8216
  9.2 0.0 copy-done.2
  9.2 0.0 copy-done.5
  9.2 0.5 %prep.1 = (f32[16,8,128]{2,1,0:T(8,128)S(1)}, f32[16,8,128]{2,1,0:T(8,128)S(1)}, f32[16,8,128]{2,1,0:T(8,128)S(1)}, f32[4,8,128]{2,1,0:T(8,128)S(1)}, bf16[32,64...) custom-call(s32[16,128]{1,0:T(8,128)S(1)} %bitcast.12, ...), custom_call_target="tpu_custom_call" | custom-call | flops 67108864 | bytes 1048576 | tf_op jit(solution)/shard_map/prep/pallas_call | solution.py:407
  9.8 1.3 %collective-permute-done.two_ref = f32[33,8,128]{2,1,0:T(8,128)S(1)} collective-permute-done((f32[33,8,128]{2,1,0:T(8,128)S(1)}, f32[33,8,128]{2,1,0:T(8,128)S(1)}, u32[]{:S(2)}, u32[]{:S(2)}) %collective-permute-start) | collective-permute-done | bytes 135200 | tf_op jit(solution)/shard_map/ppermute | solution.py:402
  11.0 2.5 %collective-permute-done.1.one_ref = f32[33,8,128]{2,1,0:T(8,128)S(1)} collective-permute-done((f32[33,8,128]{2,1,0:T(8,128)S(1)}, f32[33,8,128]{2,1,0:T(8,128)S(1)}, u32[]{:S(2)}, u32[]{:S(2)}) %collective-permute-start.1) | collective-permute-done | bytes 135200 | tf_op jit(solution)/shard_map/ppermute | solution.py:402
  13.5 0.1 columns.1
  13.6 9.4 %collective-permute-start.3 = (f32[10,8,128]{2,1,0:T(8,128)S(1)}, f32[10,8,128]{2,1,0:T(8,128)S(1)}, u32[]{:S(2)}, u32[]{:S(2)}) collective-permute-start(f32[10,8,128]{2,1,0:T(8,128)S(1)} %columns.1), channel_id=1, source_target_pairs={{16,32},{32,16},{48,64},{64,48},{80,96},{96,80},{112,128},{128,112... | collective-permute-start | bytes 122888 | tf_op jit(solution)/shard_map/ppermute | solution.py:402
  23.0 1.9 %collective-permute-start.2 = (f32[10,8,128]{2,1,0:T(8,128)S(1)}, f32[10,8,128]{2,1,0:T(8,128)S(1)}, u32[]{:S(2)}, u32[]{:S(2)}) collective-permute-start(f32[10,8,128]{2,1,0:T(8,128)S(1)} %columns.1), channel_id=1, source_target_pairs={{0,16},{16,0},{32,48},{48,32},{64,80},{80,64},{96,112},{112,96},{1... | collective-permute-start | bytes 122888 | tf_op jit(solution)/shard_map/ppermute | solution.py:402
  25.0 0.0 collective-permute-done.3.second_ref
  25.0 1.2 %collective-permute-done.2.first_ref = f32[10,8,128]{2,1,0:T(8,128)S(1)} collective-permute-done((f32[10,8,128]{2,1,0:T(8,128)S(1)}, f32[10,8,128]{2,1,0:T(8,128)S(1)}, u32[]{:S(2)}, u32[]{:S(2)}) %collective-permute-start.2) | collective-permute-done | bytes 40992 | tf_op jit(solution)/shard_map/ppermute | solution.py:402
  26.1 3.2 %main.1 = (f32[16,8,128]{2,1,0:T(8,128)}, f32[16,8,128]{2,1,0:T(8,128)}, f32[32,128]{1,0:T(8,128)S(1)}) custom-call(f32[16,8,128]{2,1,0:T(8,128)S(1)} %get-tuple-element.22.t_ref, f32[16,8,128]{2,1,0:T(8,128)S(1)} %get-tuple-element.23.s_ref, f32[16,8,128]{2,1,0:T(8,128)S(1)} %get-tuple-element.24.u_ref, f32[16,8,128]{2,1,0:T(8,128)S(1)} %get-tuple-element.25.v_ref, ...), custom_call_target="tpu_custom_call" | custom-call | flops 16777216 | bytes 1048576 | tf_op jit(solution)/shard_map/main/pallas_call | solution.py:434
  29.4 14.2 %all_to_all.5 = f32[32,1,128]{2,1,0:T(1,128)S(1)} all-to-all(f32[32,1,128]{2,1,0:T(1,128)S(1)} %bitcast.11), channel_id=1, replica_groups={{272,288,304,320,336,352,368,384,400,416,432,448,464,480,496,0,16,32,48..., dimensions={0} | all-to-all | bytes 32768 | tf_op jit(solution)/shard_map/all_to_all | solution.py:443
  43.5 0.9 %owner.1 = f32[2,1,256]{2,1,0:T(1,128)} custom-call(f32[32,128]{1,0:T(8,128)S(1)} %bitcast.9), custom_call_target="tpu_custom_call" | custom-call | flops 1048576 | bytes 1048576 | tf_op jit(solution)/shard_map/owner/pallas_call | solution.py:444
Async XLA Ops:
  0.6 7.9 %copy-start = (f32[15,8,128]{2,1,0:T(8,128)S(1)}, f32[15,8,128]{2,1,0:T(8,128)}, u32[]{:S(2)}) copy-start(f32[15,8,128]{2,1,0:T(8,128)} %mix_ref.1) | copy-start | bytes 184324
  0.6 7.9 %copy-start.1 = (s32[1,8192]{1,0:T(1,128)S(1)}, s32[1,8192]{1,0:T(1,128)}, u32[]{:S(2)}) copy-start(s32[1,8192]{1,0:T(1,128)} %param.23) | copy-start | bytes 98308
  0.7 7.9 %copy-start.4 = (s32[1,2048]{1,0:T(1,128)S(1)}, s32[1,2048]{1,0:T(1,128)}, u32[]{:S(2)}) copy-start(s32[1,2048]{1,0:T(1,128)} %param.21) | copy-start | bytes 24580
  1.7 9.3 %collective-permute-start = (f32[33,8,128]{2,1,0:T(8,128)S(1)}, f32[33,8,128]{2,1,0:T(8,128)S(1)}, u32[]{:S(2)}, u32[]{:S(2)}) collective-permute-start(f32[33,8,128]{2,1,0:T(8,128)S(1)} %get-tuple-element.29), channel_id=1, source_target_pairs={{1,2},{2,1},{3,4},{4,3},{5,6},{6,5},{7,8},{8,7},{9,10},{10,9},{11,... | collective-permute-start | bytes 405512 | tf_op jit(solution)/shard_map/ppermute | solution.py:402
  6.6 6.9 %collective-permute-start.1 = (f32[33,8,128]{2,1,0:T(8,128)S(1)}, f32[33,8,128]{2,1,0:T(8,128)S(1)}, u32[]{:S(2)}, u32[]{:S(2)}) collective-permute-start(f32[33,8,128]{2,1,0:T(8,128)S(1)} %get-tuple-element.30), channel_id=1, source_target_pairs={{0,1},{1,0},{2,3},{3,2},{4,5},{5,4},{6,7},{7,6},{8,9},{9,8},{10,11... | collective-permute-start | bytes 405512 | tf_op jit(solution)/shard_map/ppermute | solution.py:402
  8.5 0.7 %copy-start.3 = (s32[1,2048]{1,0:T(1,128)S(1)}, s32[1,2048]{1,0:T(1,128)}, u32[]{:S(2)}) copy-start(s32[1,2048]{1,0:T(1,128)} %param.20) | copy-start | bytes 24580
  8.5 0.7 %copy-start.2 = (s32[1,2048]{1,0:T(1,128)S(1)}, s32[1,2048]{1,0:T(1,128)}, u32[]{:S(2)}) copy-start(s32[1,2048]{1,0:T(1,128)} %param.19) | copy-start | bytes 24580
  8.5 0.7 %copy-start.5 = (f32[64]{0:T(128)S(1)}, f32[64]{0:T(128)}, u32[]{:S(2)}) copy-start(f32[64]{0:T(128)} %param.22) | copy-start | bytes 772
  13.6 11.3 %collective-permute-start.3 = (f32[10,8,128]{2,1,0:T(8,128)S(1)}, f32[10,8,128]{2,1,0:T(8,128)S(1)}, u32[]{:S(2)}, u32[]{:S(2)}) collective-permute-start(f32[10,8,128]{2,1,0:T(8,128)S(1)} %columns.1), channel_id=1, source_target_pairs={{16,32},{32,16},{48,64},{64,48},{80,96},{96,80},{112,128},{128,112... | collective-permute-start | bytes 122888 | tf_op jit(solution)/shard_map/ppermute | solution.py:402
  23.0 3.1 %collective-permute-start.2 = (f32[10,8,128]{2,1,0:T(8,128)S(1)}, f32[10,8,128]{2,1,0:T(8,128)S(1)}, u32[]{:S(2)}, u32[]{:S(2)}) collective-permute-start(f32[10,8,128]{2,1,0:T(8,128)S(1)} %columns.1), channel_id=1, source_target_pairs={{0,16},{16,0},{32,48},{48,32},{64,80},{80,64},{96,112},{112,96},{1... | collective-permute-start | bytes 122888 | tf_op jit(solution)/shard_map/ppermute | solution.py:402
